TPU v7x, 256 devices: a whole 4x4x8 slice. The times are simulated.
256 devices in a mesh: grp: 16 (over z_lo, x, core), peak: 16 (over y, z_hi).
Axes of the slice: x: 4, y: 4, z: 8 (z_hi: 4, z_lo: 2; z = z_hi * 2 + z_lo), core: 2. Of those that a mesh axis runs over, the one named last changes fastest.
Arguments:
- counts: bfloat16 [1024, 524288], P(None, ('grp', 'peak')), may hold values from 0.099609375 to 4
- tile_mask: int32 [1024, 4096], P(None, ('grp', 'peak')), may hold values 0 or 1
- neighbours: int32 [1024, 15], P(('grp', 'peak')), may hold values from 0 to 1023, as said below
- peak_weight: bfloat16 [524288, 512], P(('grp', 'peak')), may hold values from -0.013671875 to 0.013671875
- gain: float32 [512], replicated, may hold values from 0.25 to 1.75
- w_in: bfloat16 [512, 512], replicated, may hold values from -0.25 to 0.25
- w_out: bfloat16 [512, 256], replicated, may hold values from -0.25 to 0.25
Outputs:
- peak_grad: float32 [524288, 512], P(('grp', 'peak'))
- gain_grad: float32 [512], replicated
- in_grad: float32 [512, 512], replicated
- out_grad: float32 [512, 256], replicated
Inputs may be any that keep to these rules, and one draw needn't show every extreme that they name: `neighbours`: every entry is a cell index other than its own row's cell.
All inputs are finite; a program needn't handle non-finite values. No bound on the sum of `tile_mask` on one device may be relied on, other than what follows from the above.
Results may differ from a plain program's by a relative error of at most 0.012.
Values may be sent and summed in bfloat16 or wider, within the bound.
A program may use at most 64 MiB of HBM per device.

v0:
```python
import jax
import jax.numpy as jnp
from jax import lax
from jax.sharding import PartitionSpec as P

TILE = 128
K = 15


sharpness_divisor = 0.2
eps_norm = 1e-06
gelu_coef = 0.7978845608
cubic_coef = 0.044715


def gelu_tanh(values):
    return (
        0.5
        * values
        * (1.0 + jnp.tanh(gelu_coef * (values + cubic_coef * values * values * values)))
    )


def gelu_slope(values):
    tangent = jnp.tanh(gelu_coef * (values + cubic_coef * values * values * values))
    return 0.5 * (1.0 + tangent) + 0.5 * values * (1.0 - tangent * tangent) * gelu_coef * (
        1.0 + 3.0 * cubic_coef * values * values
    )


def collapsed_lines(left, right):
    return lax.dot_general(
        left, right, (((0,), (0,)), ((), ())), preferred_element_type=jnp.float32
    )


def tower_forward(hidden, gain, w_in, w_out):
    scale = lax.rsqrt(jnp.mean(hidden * hidden, axis=1, keepdims=True) + eps_norm)
    normed = hidden * scale
    rounded = (normed * gain[None, :]).astype(jnp.bfloat16)
    preact = jnp.dot(rounded, w_in, preferred_element_type=jnp.float32)
    activ = gelu_tanh(preact).astype(jnp.bfloat16)
    project = jnp.dot(activ, w_out, preferred_element_type=jnp.float32)
    length = lax.rsqrt(jnp.sum(project * project, axis=1, keepdims=True) + eps_norm)
    unit = project * length
    return ((scale, normed, rounded, preact, activ, length, unit), unit.astype(jnp.bfloat16))


def tower_backward(vector_derivative, gain, w_in, w_out, saved):
    scale, normed, rounded, preact, activ, length, unit = saved
    dproj = (
        length
        * (vector_derivative - unit * jnp.sum(unit * vector_derivative, axis=1, keepdims=True))
    ).astype(jnp.bfloat16)
    out_grad = collapsed_lines(activ, dproj)
    dact = jnp.dot(dproj, w_out.T, preferred_element_type=jnp.float32)
    dpre = (dact * gelu_slope(preact)).astype(jnp.bfloat16)
    in_grad = collapsed_lines(rounded, dpre)
    dround = jnp.dot(dpre, w_in.T, preferred_element_type=jnp.float32)
    gain_grad = jnp.sum(dround * normed, axis=0)
    dnorm = dround * gain[None, :]
    dhidden = scale * (dnorm - normed * jnp.mean(dnorm * normed, axis=1, keepdims=True))
    return (dhidden.astype(jnp.bfloat16), gain_grad, in_grad, out_grad)


def count_lists(lists, column_ids):
    tallies = jnp.zeros((lists.shape[0], column_ids.shape[1]), jnp.float32)
    for slot in range(lists.shape[1]):
        tallies = tallies + (lists[:, slot][:, None] == column_ids).astype(jnp.float32)
    return tallies


def body(counts, tile_mask, neighbours, peak_weight, gain, w_in, w_out):
    total_cells = counts.shape[0]
    own_rows = neighbours.shape[0]
    position = lax.axis_index(("grp", "peak"))
    first_row = position * own_rows
    masked = counts * jnp.repeat(tile_mask.astype(jnp.bfloat16), TILE, axis=1)
    whole_term = jnp.dot(masked, peak_weight, preferred_element_type=jnp.float32)
    hidden = lax.psum_scatter(whole_term, ("grp", "peak"), scatter_dimension=0, tiled=True)
    saved, sample_vectors = tower_forward(hidden, gain, w_in, w_out)
    codes_whole = lax.all_gather(sample_vectors, ("grp", "peak"), axis=0, tiled=True)
    affinity_scores = (
        jnp.einsum("ce,ke->ck", sample_vectors, codes_whole, preferred_element_type=jnp.float32)
        / sharpness_divisor
    )
    row_ids = lax.broadcasted_iota(jnp.int32, (own_rows, total_cells), 0) + first_row
    col_ids = lax.broadcasted_iota(jnp.int32, (own_rows, total_cells), 1)
    expo = jnp.where(row_ids == col_ids, jnp.float32(0.0), jnp.exp(affinity_scores))
    row_total = jnp.sum(expo, axis=1, keepdims=True)
    prob = expo / row_total
    neighbour_coefficients = (prob - count_lists(neighbours, col_ids) / K).astype(jnp.bfloat16)
    source_portion = jnp.dot(
        neighbour_coefficients, codes_whole, preferred_element_type=jnp.float32
    )
    target_portion = lax.psum_scatter(
        collapsed_lines(neighbour_coefficients, sample_vectors),
        ("grp", "peak"),
        scatter_dimension=0,
        tiled=True,
    )
    vector_derivative = (source_portion + target_portion) / sharpness_divisor
    dhidden, gain_part, in_part, out_part = tower_backward(
        vector_derivative, gain, w_in, w_out, saved
    )
    gain_grad, in_grad, out_grad = lax.psum((gain_part, in_part, out_part), ("grp", "peak"))
    dhidden_whole = lax.all_gather(dhidden, ("grp", "peak"), axis=0, tiled=True)
    peak_grad = collapsed_lines(masked, dhidden_whole)
    return (peak_grad, gain_grad, in_grad, out_grad)


def solution(mesh):
    placed = (
        P(None, ("grp", "peak")),
        P(None, ("grp", "peak")),
        P(("grp", "peak"), None),
        P(("grp", "peak"), None),
        P(),
        P(),
        P(),
    )
    return jax.shard_map(
        body,
        mesh=mesh,
        in_specs=placed,
        out_specs=(P(("grp", "peak"), None), P(), P(), P()),
        check_vma=False,
    )
```

profile of v0, /device:TPU:1, one launch (start us, length us, event | category | flops | bytes accessed | tf_op | source)
XLA Modules:
  0.0 2082.9 jit_solution(7782951324887230128)
XLA Ops:
  7.2 0.0 copy-start
  7.2 0.0 all-reduce.7.cloned.1.call-start
  7.2 1.0 convert_element_type.69
  8.2 0.2 copy.12
  8.4 0.0 copy-start.6
  8.4 4.5 broadcast_in_dim.6
  12.9 0.0 copy-start.1
  12.9 1.9 copy-done.1
  14.8 0.0 copy-done
  14.8 0.0 copy-done.6
  14.8 0.0 copy-start.5
  14.8 0.0 copy-start.4
  14.8 3.7 fusion.5
  18.5 0.0 all-reduce.7.cloned.1.call-update
  18.5 0.0 all-reduce.9.cloned.1.call-start
  18.6 0.0 copy-done.3
  18.6 0.4 slice_reduce_fusion.14
  19.0 263.2 %all-reduce.7.cloned.1.call-done = f32[1024,512]{1,0:T(8,128)} async-done(((f32[1024,512]{1,0:T(8,128)}), f32[1024,512]{1,0:T(8,128)}) %all-reduce.7.cloned.1.call-update) | async-done | bytes 2097168
  282.2 0.8 multiply_reduce_fusion.2
  283.1 0.0 copy-done.2
  283.1 0.0 copy-done.5
  283.1 0.9 fusion.14
  284.0 0.0 copy-done.4
  284.0 0.3 multiply_reduce_fusion.4
  284.3 0.1 fusion.33
  284.4 606.8 %all-gather = bf16[256,4,256]{2,1,0:T(4,128)(2,1)S(1)} all-gather(bf16[1,4,256]{2,1,0:T(4,128)(2,1)S(1)} %fusion.33), channel_id=1, replica_groups=mesh['grp'=16,'peak'=16] {'grp','peak'}, dimensions={0}, use_global_device_ids=true | all-gather | bytes 526336 | tf_op jit(solution)/shard_map/all_gather | solution.py:82
  891.1 0.9 reshape.34
  892.0 1.4 fusion.20
  893.4 1.4 fusion.17
  894.9 0.0 all-reduce.9.cloned.1.call-update
  894.9 0.0 all-gather.4.cloned.1.call-start
  894.9 382.4 %all-reduce.9.cloned.1.call-done = f32[1024,256]{1,0:T(8,128)} async-done(((f32[1024,256]{1,0:T(8,128)}), f32[1024,256]{1,0:T(8,128)}) %all-reduce.9.cloned.1.call-update) | async-done | bytes 1048592
  1277.3 1.4 multiply_reduce_fusion.3
  1278.7 0.2 fusion.2
  1278.9 1.1 multiply_reduce_fusion
  1280.0 1.4 fusion.12
  1281.4 0.0 all-gather.4.cloned.1.call-update
  1281.4 0.0 all-reduce.11.cloned.1.call-start
  1281.5 77.5 %psum.21 = f32[512]{0:T(512)} all-reduce(f32[512]{0:T(512)S(1)} %get-tuple-element.4), channel_id=1, replica_groups=mesh['grp'=16,'peak'=16] {'grp','peak'}, use_global_device_ids=true, to_apply=%region_8.9 | all-reduce | flops 512 | bytes 4096 | tf_op jit(solution)/shard_map/psum | solution.py:106
  1359.0 1.1 fusion.15
  1360.1 2.1 fusion.13
  1362.2 0.0 all-reduce.11.cloned.1.call-update
  1362.2 449.5 %all-gather.4.cloned.1.call-done = bf16[256,4,512]{2,1,0:T(4,128)(2,1)} async-done(((bf16[1,4,512]{2,1,0:T(4,128)(2,1)}), bf16[256,4,512]{2,1,0:T(4,128)(2,1)}) %all-gather.4.cloned.1.call-update) | async-done | bytes 1048592 | tf_op jit(solution)/shard_map/all_gather | solution.py:107
  1811.8 1.3 reshape.36
  1813.1 8.1 fusion.4
  1821.2 251.0 %all-reduce.11.cloned.1.call-done = (f32[512,512]{1,0:T(8,128)}, f32[512,256]{1,0:T(8,128)}) async-done(((f32[512,512]{1,0:T(8,128)}, f32[512,256]{1,0:T(8,128)}), (f32[512,512]{1,0:T(8,128)}, f32[512,256]{1,0:T(8,128)})) %all-reduce.11.cloned.1.call-update) | async-done | bytes 1572880 | tf_op jit(solution)/shard_map/psum | solution.py:106
  2072.2 2.3 copy.21
  2074.5 1.9 copy.22
  (6 shorter events, 0.0 us)
Async XLA Ops:
  7.2 7.6 copy-start
  7.2 275.0 %all-reduce.7.cloned.1.call-start = ((), (), s32[]{:S(2)}) async-start(), calls=%async_computation.1 | async-start | bytes 4194304
  8.4 6.4 copy-start.6
  12.9 1.9 copy-start.1
  14.8 3.8 copy-start.3
  14.8 268.2 %copy-start.2 = (bf16[512,512]{1,0:T(8,128)(2,1)S(1)}, bf16[512,512]{1,0:T(8,128)(2,1)}, u32[]{:S(2)}) copy-start(bf16[512,512]{1,0:T(8,128)(2,1)} %param.12) | copy-start | bytes 1572868
  14.8 268.2 %copy-start.5 = (f32[512]{0:T(512)S(1)}, f32[512]{0:T(512)}, u32[]{:S(2)}) copy-start(f32[512]{0:T(512)} %param.11) | copy-start | bytes 6148
  14.8 269.2 %copy-start.4 = (bf16[512,256]{1,0:T(8,128)(2,1)S(1)}, bf16[512,256]{1,0:T(8,128)(2,1)}, u32[]{:S(2)}) copy-start(bf16[512,256]{1,0:T(8,128)(2,1)} %param.13) | copy-start | bytes 786436
  18.5 1258.8 %all-reduce.9.cloned.1.call-start = ((), (), s32[]{:S(2)}) async-start(), calls=%async_computation.2 | async-start | bytes 2097152
  894.9 916.9 %all-gather.4.cloned.1.call-start = ((), (), s32[]{:S(2)}) async-start(), calls=%async_computation | async-start | bytes 1052672 | tf_op jit(solution)/shard_map/all_gather | solution.py:107
  1281.4 790.8 %all-reduce.11.cloned.1.call-start = ((), (), s32[]{:S(2)}) async-start(), calls=%async_computation.3 | async-start | bytes 3145728 | tf_op jit(solution)/shard_map/psum | solution.py:106
Sparse Core Ops, SparseCore 0:
  18.6 263.5 all-reduce.6
  895.0 382.2 all-reduce.8
  1281.6 530.1 all-gather.3
  1818.5 253.6 all-reduce.10
where the time goes:
time: 2080 us
  waiting for transfers between devices  1350 us (65%)
  blocking collectives  684 us (33%)
  matrix products  21.7 us (1%)
    unnamed x6, waiting for transfers between devices  646 us
    all_gather x1, blocking collectives, body(): lax.all_gather(sample_vectors, ('grp', 'peak'), axis=0, tiled=True)  607 us
    all_gather x1, waiting for transfers between devices, body(): dhidden_whole = lax.all_gather(dhidden, ('grp', 'peak'), axis=0, tiled=True)  450 us
    psum x1, waiting for transfers between devices, body(): lax.psum((gain_part, in_part, out_part), ('grp', 'peak'))  251 us
    psum x1, blocking collectives, body(): lax.psum((gain_part, in_part, out_part), ('grp', 'peak'))  77.5 us
  transfers between devices with their start and end apart: 4, of which 4 were waited for; matrix products, arithmetic and copies ran while one was open for 1% of the time, Pallas kernels for 0%

commit v1 on v0

v1 whole, which is shorter than its diff:
```python
import jax
import jax.numpy as jnp
from jax import lax
from jax.experimental import pallas as pl
from jax.experimental.pallas import tpu as pltpu
from jax.sharding import PartitionSpec as P

TILE = 128
K = 15
CELLS = 1024
D = 512
HID = 512
E = 256
LOCAL = 2048
HALF = CELLS // 2
PIECE = HALF // 16
BLOCK = 256
SLOT = 16

sharpness = 5.0
eps_norm = 1e-06
gelu_coef = 0.7978845608
cubic_coef = 0.044715

bf16 = jnp.bfloat16
f32 = jnp.float32
i32 = jnp.int32
MESH = pl.DeviceIdType.MESH


def coordinates():
    grp = lax.axis_index("grp")
    peak = lax.axis_index("peak")
    return (grp // 2) % 4, peak // 4, (peak % 4) * 2 + grp // 8, grp % 2


def device(x, y, z, core):
    return {"grp": ((z % 2) * 4 + x) * 2 + core, "peak": y * 4 + z // 2}


def rows_of(start, size):
    return pl.ds(pl.multiple_of(start, size), size)


def gather_kernel(
    counts, tile_mask, neighbours, weight,
    hidden_out, turned_out, tallies_out,
    loaded, masked, turned, w_buf, partial, core_send, core_recv, plane_send, plane_recv,
    column, hidden, lists, list_rows, counted, tallies,
    load_sem, w_sem, core_ss, core_rs, plane_ss, plane_rs, z_ss, z_rs,
    out_ss, out_rs, fwd_ss, fwd_rs, list_ss, list_rs, store_sem,
):
    x, y, z, core = coordinates()
    plane = x * 4 + y
    sibling = device(x, y, z, 1 - core)

    def plane_at(step):
        return (x + step // 4) % 4, (y + step % 4) % 4

    def plane_from(step):
        return (x + 4 - step // 4) % 4, (y + 4 - step % 4) % 4

    barrier = pltpu.get_barrier_semaphore()
    pl.semaphore_signal(barrier, inc=1, device_id=sibling, device_id_type=MESH)

    def greet_plane(step, carry):
        px, py = plane_at(step)
        pl.semaphore_signal(barrier, inc=1, device_id=device(px, py, z, core), device_id_type=MESH)
        return carry

    def greet_column(step, carry):
        pl.semaphore_signal(
            barrier, inc=1, device_id=device(x, y, (z + step) % 8, core), device_id_type=MESH
        )
        return carry

    lax.fori_loop(1, 16, greet_plane, 0)
    lax.fori_loop(1, 8, greet_column, 0)

    def block_start(step):
        return HALF * ((1 - core + step // 2) % 2) + BLOCK * (step % 2)

    def load(step):
        rows = rows_of(block_start(step), BLOCK)
        return pltpu.make_async_copy(counts.at[rows], loaded.at[rows], load_sem.at[step])

    w_copy = pltpu.make_async_copy(weight, w_buf, w_sem)
    w_copy.start()
    for step in range(4):
        load(step).start()

    own_slot = (z * 16 + plane) * 2 + core
    lists[own_slot] = jnp.zeros((1, 128), i32)
    for cell in range(4):
        lists[own_slot, :, cell * SLOT : cell * SLOT + K] = neighbours[cell : cell + 1, :]

    def list_core():
        return pltpu.make_async_remote_copy(
            src_ref=lists.at[own_slot], dst_ref=lists.at[own_slot],
            send_sem=list_ss.at[0], recv_sem=list_rs.at[0],
            device_id=sibling, device_id_type=MESH,
        )

    def list_plane(step):
        px, py = plane_at(step)
        part = lists.at[pl.ds((z * 16 + plane) * 2, 2)]
        return pltpu.make_async_remote_copy(
            src_ref=part, dst_ref=part,
            send_sem=list_ss.at[step], recv_sem=list_rs.at[step],
            device_id=device(px, py, z, core), device_id_type=MESH,
        )

    def list_column(step):
        part = lists.at[pl.ds(z * 32, 32)]
        return pltpu.make_async_remote_copy(
            src_ref=part, dst_ref=part,
            send_sem=list_ss.at[15 + step], recv_sem=list_rs.at[15 + step],
            device_id=device(x, y, (z + step) % 8, core), device_id_type=MESH,
        )

    def core_copy(step):
        rows = rows_of(BLOCK * step, BLOCK)
        return pltpu.make_async_remote_copy(
            src_ref=core_send.at[rows], dst_ref=core_recv.at[rows],
            send_sem=core_ss.at[step], recv_sem=core_rs.at[step],
            device_id=sibling, device_id_type=MESH,
        )

    def plane_copy(step):
        px, py = plane_at(step)
        return pltpu.make_async_remote_copy(
            src_ref=plane_send.at[rows_of((px * 4 + py) * PIECE, PIECE)], dst_ref=plane_recv.at[step],
            send_sem=plane_ss.at[step], recv_sem=plane_rs.at[step],
            device_id=device(px, py, z, core), device_id_type=MESH,
        )

    def column_copy(step):
        return pltpu.make_async_remote_copy(
            src_ref=column.at[z], dst_ref=column.at[z],
            send_sem=z_ss.at[step], recv_sem=z_rs.at[step],
            device_id=device(x, y, (z + step) % 8, core), device_id_type=MESH,
        )

    own_rows = rows_of(core * HALF + plane * PIECE, PIECE)

    def out_copy(step):
        px, py = plane_at(step)
        return pltpu.make_async_remote_copy(
            src_ref=hidden.at[own_rows], dst_ref=hidden.at[own_rows],
            send_sem=out_ss.at[step], recv_sem=out_rs.at[step],
            device_id=device(px, py, z, core), device_id_type=MESH,
        )

    def fwd_copy(step):
        px, py = plane_from(step)
        rows = rows_of(core * HALF + (px * 4 + py) * PIECE, PIECE)
        return pltpu.make_async_remote_copy(
            src_ref=hidden.at[rows], dst_ref=hidden.at[rows],
            send_sem=fwd_ss.at[step], recv_sem=fwd_rs.at[step],
            device_id=sibling, device_id_type=MESH,
        )

    def each(first, last, what):
        def run(step, carry):
            what(step)
            return carry

        lax.fori_loop(first, last, run, 0)

    pl.semaphore_wait(barrier, 23)
    list_core().start()
    w_copy.wait()

    def peak_block(step, carry):
        start = block_start(step)
        rows = rows_of(start, BLOCK)
        load(step).wait()
        keep = tile_mask[rows, :].astype(f32).astype(bf16)
        for tile in range(LOCAL // TILE):
            lanes = slice(tile * TILE, (tile + 1) * TILE)
            masked[rows, lanes] = loaded[rows, lanes] * jnp.broadcast_to(
                keep[:, tile : tile + 1], (BLOCK, TILE)
            )
        term = jnp.dot(masked[rows, :], w_buf[...], preferred_element_type=f32)

        @pl.when(step < 2)
        def _():
            core_send[rows_of(BLOCK * step, BLOCK), :] = term.astype(bf16)
            core_copy(step).start()

        @pl.when(step >= 2)
        def _():
            partial[rows_of(BLOCK * (step - 2), BLOCK), :] = term

        return carry

    lax.fori_loop(0, 4, peak_block, 0)

    list_core().wait()
    each(1, 16, lambda step: list_plane(step).start())
    for step in range(2):
        core_copy(step).wait()
    for part in range(4):
        rows = slice(part * 128, (part + 1) * 128)
        plane_send[rows, :] = (partial[rows, :] + core_recv[rows, :].astype(f32)).astype(bf16)
    each(1, 16, lambda step: plane_copy(step).start())
    each(1, 16, lambda step: list_plane(step).wait())
    each(1, 8, lambda step: list_column(step).start())

    def turn(step, carry):
        rows = rows_of(step * 128, 128)
        for tile in range(LOCAL // TILE):
            lanes = slice(tile * TILE, (tile + 1) * TILE)
            turned[lanes, rows] = masked[rows, lanes].T
        return carry

    lax.fori_loop(0, CELLS // 128, turn, 0)
    turned_store = pltpu.make_async_copy(turned, turned_out, store_sem.at[0])
    turned_store.start()

    def add_plane(step, total):
        plane_copy(step).wait()
        return total + plane_recv[step].astype(f32)

    total = lax.fori_loop(1, 16, add_plane, plane_send[rows_of(plane * PIECE, PIECE), :].astype(f32))
    column[z] = total.astype(bf16)
    each(1, 8, lambda step: column_copy(step).start())
    each(1, 8, lambda step: list_column(step).wait())

    by_slot = lists[:, 0, :].astype(f32).T
    place = lax.broadcasted_iota(i32, (CELLS // 4, 1), 0)
    at_core, at_y, at_x, at_z = place % 2, (place // 2) % 4, (place // 8) % 4, place // 32
    holder = (((at_z % 2) * 4 + at_x) * 2 + at_core) * 16 + at_y * 4 + at_z // 2
    cells = lax.broadcasted_iota(i32, (CELLS // 4, CELLS), 1)
    gathered = jnp.zeros((2 * SLOT, CELLS), f32)
    for cell in range(4):
        chosen = (holder * 4 + cell == cells).astype(f32).astype(bf16)
        entry = by_slot[cell * SLOT : (cell + 1) * SLOT, :]
        high = jnp.floor(entry * (1.0 / 32.0))
        low = entry - 32.0 * high
        gathered += jnp.dot(
            jnp.concatenate([high, low], axis=0).astype(bf16), chosen, preferred_element_type=f32
        )
    list_rows[...] = 32.0 * gathered[:SLOT, :] + gathered[SLOT:, :]

    for part in range(CELLS // 128):
        lanes = slice(part * 128, (part + 1) * 128)

        def count(step, carry):
            ids = (lax.broadcasted_iota(i32, (64, 128), 0) + step * 64).astype(f32)
            total = jnp.zeros((64, 128), f32)
            for slot in range(K):
                total += jnp.where(list_rows[slot : slot + 1, lanes] == ids, 1.0, 0.0)
            counted[rows_of(step * 64, 64), lanes] = total.astype(bf16)
            return carry

        lax.fori_loop(0, CELLS // 64, count, 0)

    each(1, 8, lambda step: column_copy(step).wait())
    whole = column[0].astype(f32)
    for step in range(1, 8):
        whole += column[step].astype(f32)
    hidden[own_rows, :] = whole.astype(bf16)
    each(1, 16, lambda step: out_copy(step).start())
    fwd_copy(0).start()

    def both(step, carry):
        rows = rows_of(step * 128, 128)
        for part in range(CELLS // 128):
            lanes = slice(part * 128, (part + 1) * 128)
            tallies[rows, lanes] = counted[rows, lanes] + counted[lanes, rows].T
        return carry

    lax.fori_loop(0, CELLS // 128, both, 0)
    tallies_store = pltpu.make_async_copy(tallies, tallies_out, store_sem.at[1])
    tallies_store.start()

    def pass_on(step):
        out_copy(step).wait()
        fwd_copy(step).start()

    each(1, 16, pass_on)
    each(0, 16, lambda step: fwd_copy(step).wait())
    hidden_store = pltpu.make_async_copy(hidden, hidden_out, store_sem.at[2])
    hidden_store.start()
    hidden_store.wait()
    turned_store.wait()
    tallies_store.wait()


def gather_hidden(counts, tile_mask, neighbours, weight):
    any_space = pl.BlockSpec(memory_space=pl.ANY)
    vmem = pl.BlockSpec(memory_space=pltpu.VMEM)
    dma = pltpu.SemaphoreType.DMA
    return pl.pallas_call(
        gather_kernel,
        name="gather_hidden",
        out_shape=(
            jax.ShapeDtypeStruct((CELLS, D), bf16),
            jax.ShapeDtypeStruct((LOCAL, CELLS), bf16),
            jax.ShapeDtypeStruct((CELLS, CELLS), bf16),
        ),
        in_specs=[any_space, vmem, vmem, any_space],
        out_specs=(any_space, any_space, any_space),
        scratch_shapes=[
            pltpu.VMEM((CELLS, LOCAL), bf16),
            pltpu.VMEM((CELLS, LOCAL), bf16),
            pltpu.VMEM((LOCAL, CELLS), bf16),
            pltpu.VMEM((LOCAL, D), bf16),
            pltpu.VMEM((HALF, D), f32),
            pltpu.VMEM((HALF, D), bf16),
            pltpu.VMEM((HALF, D), bf16),
            pltpu.VMEM((HALF, D), bf16),
            pltpu.VMEM((16, PIECE, D), bf16),
            pltpu.VMEM((8, PIECE, D), bf16),
            pltpu.VMEM((CELLS, D), bf16),
            pltpu.VMEM((CELLS // 4, 1, 128), i32),
            pltpu.VMEM((SLOT, CELLS), f32),
            pltpu.VMEM((CELLS, CELLS), bf16),
            pltpu.VMEM((CELLS, CELLS), bf16),
            dma((4,)), dma, dma((2,)), dma((2,)), dma((16,)), dma((16,)), dma((8,)), dma((8,)),
            dma((16,)), dma((16,)), dma((16,)), dma((16,)), dma((23,)), dma((23,)), dma((3,)),
        ],
        compiler_params=pltpu.CompilerParams(
            collective_id=0, has_side_effects=True, vmem_limit_bytes=48 << 20
        ),
        cost_estimate=pl.CostEstimate(
            flops=2 * CELLS * LOCAL * D, bytes_accessed=16 << 20, transcendentals=0
        ),
    )(counts, tile_mask, neighbours, weight)


def across(left, right):
    return lax.dot_general(left, right, (((1,), (1,)), ((), ())), preferred_element_type=f32)


def collapsed(left, right):
    return lax.dot_general(left, right, (((0,), (0,)), ((), ())), preferred_element_type=f32)


def tower_kernel(
    hidden, turned, tallies, gain, w_in, w_out,
    peak_grad, gain_grad, in_grad, out_grad,
    turned_buf, tallies_buf, rounded, slope, activ, unit, length, scale, codes, expo, inverse,
    dproj, dpre, dhidden, peak_buf, load_sem, store_sem,
):
    tallies_copy = pltpu.make_async_copy(tallies, tallies_buf, load_sem.at[0])
    tallies_copy.start()
    turned_copy = pltpu.make_async_copy(turned, turned_buf, load_sem.at[1])
    turned_copy.start()

    step_rows = 256
    steps = CELLS // step_rows

    def forward(step, carry):
        rows = rows_of(step * step_rows, step_rows)
        h = hidden[rows, :].astype(f32)
        s = lax.rsqrt(jnp.mean(h * h, axis=1, keepdims=True) + eps_norm)
        scale[rows, :] = s
        r = (h * s * gain[...]).astype(bf16)
        rounded[rows, :] = r
        v = jnp.dot(r, w_in[...], preferred_element_type=f32)
        t = jnp.tanh(gelu_coef * (v + cubic_coef * v * v * v))
        a = (0.5 * v * (1.0 + t)).astype(bf16)
        activ[rows, :] = a
        slope[rows, :] = 0.5 * (1.0 + t) + 0.5 * v * (1.0 - t * t) * gelu_coef * (
            1.0 + 3.0 * cubic_coef * v * v
        )
        p = jnp.dot(a, w_out[...], preferred_element_type=f32)
        n = lax.rsqrt(jnp.sum(p * p, axis=1, keepdims=True) + eps_norm)
        length[rows, :] = n
        u = p * n
        unit[rows, :] = u
        codes[rows, :] = u.astype(bf16)
        return carry

    lax.fori_loop(0, steps, forward, 0)

    def score(step, column_total):
        rows = rows_of(step * step_rows, step_rows)
        e = jnp.exp(across(codes[rows, :], codes[...]) * sharpness)
        own = lax.broadcasted_iota(i32, (step_rows, CELLS), 0) + step * step_rows
        other = lax.broadcasted_iota(i32, (step_rows, CELLS), 1)
        e = jnp.where(own == other, 0.0, e)
        expo[rows, :] = e
        inverse[rows, :] = 1.0 / jnp.sum(e, axis=1, keepdims=True)
        return column_total + jnp.sum(e, axis=0, keepdims=True)

    column_inverse = 1.0 / lax.fori_loop(0, steps, score, jnp.zeros((1, CELLS), f32))
    tallies_copy.wait()

    def backward(step, gain_total):
        rows = rows_of(step * step_rows, step_rows)
        both = expo[rows, :] * (inverse[rows, :] + column_inverse)
        both = (both - tallies_buf[rows, :].astype(f32) * (1.0 / K)).astype(bf16)
        dcodes = jnp.dot(both, codes[...], preferred_element_type=f32) * sharpness
        u = unit[rows, :]
        dp = (length[rows, :] * (dcodes - u * jnp.sum(u * dcodes, axis=1, keepdims=True))).astype(bf16)
        dproj[rows, :] = dp
        dv = (across(dp, w_out[...]) * slope[rows, :]).astype(bf16)
        dpre[rows, :] = dv
        dround = across(dv, w_in[...])
        s = scale[rows, :]
        normed = hidden[rows, :].astype(f32) * s
        dnorm = dround * gain[...]
        dhidden[rows, :] = (
            s * (dnorm - normed * jnp.mean(dnorm * normed, axis=1, keepdims=True))
        ).astype(bf16)
        return gain_total + jnp.sum(dround * normed, axis=0, keepdims=True)

    gain_grad[...] = lax.fori_loop(0, steps, backward, jnp.zeros((1, D), f32))
    turned_copy.wait()

    def store(step):
        rows = rows_of(step * step_rows, step_rows)
        return pltpu.make_async_copy(peak_buf.at[rows], peak_grad.at[rows], store_sem.at[step])

    def peak(step, carry):
        rows = rows_of(step * step_rows, step_rows)
        peak_buf[rows, :] = jnp.dot(turned_buf[rows, :], dhidden[...], preferred_element_type=f32)
        store(step).start()
        return carry

    lax.fori_loop(0, LOCAL // step_rows, peak, 0)
    in_grad[...] = collapsed(rounded[...], dpre[...])
    out_grad[...] = collapsed(activ[...], dproj[...])

    def stored(step, carry):
        store(step).wait()
        return carry

    lax.fori_loop(0, LOCAL // step_rows, stored, 0)


def tower(hidden, turned, tallies, gain, w_in, w_out):
    any_space = pl.BlockSpec(memory_space=pl.ANY)
    vmem = pl.BlockSpec(memory_space=pltpu.VMEM)
    dma = pltpu.SemaphoreType.DMA
    return pl.pallas_call(
        tower_kernel,
        name="tower",
        out_shape=(
            jax.ShapeDtypeStruct((LOCAL, D), f32),
            jax.ShapeDtypeStruct((1, D), f32),
            jax.ShapeDtypeStruct((D, HID), f32),
            jax.ShapeDtypeStruct((HID, E), f32),
        ),
        in_specs=[vmem, any_space, any_space, vmem, vmem, vmem],
        out_specs=(any_space, vmem, vmem, vmem),
        scratch_shapes=[
            pltpu.VMEM((LOCAL, CELLS), bf16),
            pltpu.VMEM((CELLS, CELLS), bf16),
            pltpu.VMEM((CELLS, D), bf16),
            pltpu.VMEM((CELLS, HID), f32),
            pltpu.VMEM((CELLS, HID), bf16),
            pltpu.VMEM((CELLS, E), f32),
            pltpu.VMEM((CELLS, 1), f32),
            pltpu.VMEM((CELLS, 1), f32),
            pltpu.VMEM((CELLS, E), bf16),
            pltpu.VMEM((CELLS, CELLS), f32),
            pltpu.VMEM((CELLS, 1), f32),
            pltpu.VMEM((CELLS, E), bf16),
            pltpu.VMEM((CELLS, HID), bf16),
            pltpu.VMEM((CELLS, D), bf16),
            pltpu.VMEM((LOCAL, D), f32),
            dma((2,)), dma((8,)),
        ],
        compiler_params=pltpu.CompilerParams(vmem_limit_bytes=48 << 20),
        cost_estimate=pl.CostEstimate(
            flops=6 << 30, bytes_accessed=16 << 20, transcendentals=2 << 20
        ),
    )(hidden, turned, tallies, gain, w_in, w_out)


def body(counts, tile_mask, neighbours, peak_weight, gain, w_in, w_out):
    hidden, turned, tallies = gather_hidden(counts, tile_mask, neighbours, peak_weight)
    peak_grad, gain_grad, in_grad, out_grad = tower(
        hidden, turned, tallies, gain.reshape(1, D), w_in, w_out
    )
    return (peak_grad, gain_grad.reshape(D), in_grad, out_grad)


def solution(mesh):
    cells = P(("grp", "peak"), None)
    peaks = P(None, ("grp", "peak"))
    return jax.shard_map(
        body,
        mesh=mesh,
        in_specs=(peaks, peaks, cells, cells, P(), P(), P()),
        out_specs=(cells, P(), P(), P()),
        check_vma=False,
    )
```

time: 2080 us -> 64.1 us (0.03)
  waiting for transfers between devices: 1350 us -> 0 us
  blocking collectives: 684 us -> 0 us
  Pallas kernels: 0 us -> 59.8 us
  matrix products: 21.7 us -> 0 us
    unnamed x6 -> x0, waiting for transfers between devices: 646 us -> none
    all_gather x1 -> x0, blocking collectives: 607 us -> none  [body(): lax.all_gather(sample_vectors, ('grp', 'peak'), axis=0, tiled=True)]
    all_gather x1 -> x0, waiting for transfers between devices: 450 us -> none  [body(): dhidden_whole = lax.all_gather(dhidden, ('grp', 'peak'), axis=0, tiled=True)]
    psum x1 -> x0, waiting for transfers between devices: 251 us -> none  [body(): lax.psum((gain_part, in_part, out_part), ('grp', 'peak'))]
    psum x1 -> x0, blocking collectives: 77.5 us -> none  [body(): lax.psum((gain_part, in_part, out_part), ('grp', 'peak'))]
    pallas_call x0 -> x2, Pallas kernels: none -> 59.8 us  [the longest x1 44.5 us: gather_hidden(): pl.pallas_call(gather_kernel, name='gather_hidden', out_shape=(jax.ShapeD...]
    dot_general x11 -> x0, matrix products: 21.7 us -> none  [the longest x4 12.7 us: collapsed_lines(): lax.dot_general(left, right, (((0,), (0,)), ((), ())), preferred_element_...]
  transfers between devices with their start and end apart: 4 -> 0, of which waited for: 4 -> 0; matrix products, arithmetic and copies ran while one was open for 1% -> 0% of each run, Pallas kernels for 0% -> 0%
where the time goes in v1:
time: 64.1 us; the launch traced here: 63.9 us
  Pallas kernels  59.8 us (93%)
  local copies, waits for them, and re-layouts  3.37 us (5%)
  between operations  0.7 us (1%)
    pallas_call x1, Pallas kernels, gather_hidden(): pl.pallas_call(gather_kernel, name='gather_hidden', out_shape=(jax.ShapeD...  44.5 us
    pallas_call x1, Pallas kernels, tower(): pl.pallas_call(tower_kernel, name='tower', out_shape=(jax.ShapeDtypeStruc...  15.3 us
    unnamed x11, local copies, waits for them, and re-layouts  3.37 us

profile of v1, /device:TPU:1, one launch (start us, length us, event | category | flops | bytes accessed | tf_op | source)
XLA Modules:
  0.0 63.9 jit_solution(5409315111102362886)
XLA Ops:
  0.6 0.0 copy-start.1
  0.6 0.0 copy-start.4
  0.7 1.1 %copy.11.tile_mask = s32[1024,16]{1,0:T(8,128)S(1)} copy(s32[1024,16]{0,1:T(8,128)} %param.8) | data formatting | bytes 131072 | tf_op args[1]
  1.7 0.0 copy-start
  1.8 1.6 %copy-done = bf16[2048,512]{1,0:T(8,128)(2,1)S(1)} copy-done((bf16[2048,512]{1,0:T(8,128)(2,1)S(1)}, bf16[2048,512]{1,0:T(8,128)(2,1)}, u32[]{:S(2)}) %copy-start) | copy-done | bytes 2097176
  3.3 0.0 copy-start.3
  3.3 0.7 %copy-done.3 = s32[4,15]{1,0:T(4,128)S(1)} copy-done((s32[4,15]{1,0:T(4,128)S(1)}, s32[4,15]{1,0:T(4,128)}, u32[]{:S(2)}) %copy-start.3) | copy-done | bytes 264
  4.0 0.0 copy-start.2
  4.0 44.5 %gather_hidden.1 = (bf16[1024,512]{1,0:T(8,128)(2,1)S(1)}, bf16[2048,1024]{1,0:T(8,128)(2,1)}, bf16[1024,1024]{1,0:T(8,128)(2,1)S(1)}) custom-call(bf16[1024,2048]{1,0:T(8,128)(2,1)} %counts.1, s32[1024,16]{1,0:T(8,128)S(1)} %copy.11.tile_mask, s32[4,15]{1,0:T(4,128)S(1)} %copy-done.3, bf16[2048,512]{1,0:T(8,128)(2,1)S(1)} %copy-done), custom_call_target="tpu_custom_call" | custom-call | flops 2147483648 | bytes 16777216 | tf_op jit(solution)/shard_map/gather_hidden/pallas_call | solution.py:295
  48.6 0.0 copy-done.1
  48.6 0.0 copy-done.4
  48.6 0.0 copy-done.2
  48.6 15.3 %tower.1 = (f32[2048,512]{1,0:T(8,128)}, f32[1,512]{1,0:T(1,128)}, f32[512,512]{1,0:T(8,128)}, f32[512,256]{1,0:T(8,128)}) custom-call(bf16[1024,512]{1,0:T(8,128)(2,1)S(1)} %get-tuple-element.11.hidden, bf16[2048,1024]{1,0:T(8,128)(2,1)} %get-tuple-element.12.turned, bf16[1024,1024]{1,0:T(8,128)(2,1)S(1)} %get-tuple-element.13.tallies, ...), custom_call_target="tpu_custom_call" | custom-call | flops 6442450944 | bytes 16777216 | tf_op jit(solution)/shard_map/tower/pallas_call | solution.py:439
Async XLA Ops:
  0.6 48.0 %copy-start.1 = (bf16[512,512]{1,0:T(8,128)(2,1)S(1)}, bf16[512,512]{1,0:T(8,128)(2,1)}, u32[]{:S(2)}) copy-start(bf16[512,512]{1,0:T(8,128)(2,1)} %w_in.1) | copy-start | bytes 1572868
  0.6 48.0 %copy-start.4 = (f32[512]{0:T(512)S(1)}, f32[512]{0:T(512)}, u32[]{:S(2)}) copy-start(f32[512]{0:T(512)} %param.11) | copy-start | bytes 6148
  1.7 1.6 %copy-start = (bf16[2048,512]{1,0:T(8,128)(2,1)S(1)}, bf16[2048,512]{1,0:T(8,128)(2,1)}, u32[]{:S(2)}) copy-start(bf16[2048,512]{1,0:T(8,128)(2,1)} %weight.1) | copy-start | bytes 6291460
  3.3 0.7 %copy-start.3 = (s32[4,15]{1,0:T(4,128)S(1)}, s32[4,15]{1,0:T(4,128)}, u32[]{:S(2)}) copy-start(s32[4,15]{1,0:T(4,128)} %neighbours.1) | copy-start | bytes 724
  4.0 44.6 %copy-start.2 = (bf16[512,256]{1,0:T(8,128)(2,1)S(1)}, bf16[512,256]{1,0:T(8,128)(2,1)}, u32[]{:S(2)}) copy-start(bf16[512,256]{1,0:T(8,128)(2,1)} %w_out.1) | copy-start | bytes 786436

commit v2 on v1

v2 whole, which is shorter than its diff:
```python
import jax
import jax.numpy as jnp
from jax import lax
from jax.experimental import pallas as pl
from jax.experimental.pallas import tpu as pltpu
from jax.sharding import PartitionSpec as P

TILE = 128
K = 15
CELLS = 1024
D = 512
HID = 512
E = 256
LOCAL = 2048
HALF = CELLS // 2
BLOCK = 256
PIECE = BLOCK // 16
SLOT = 16

sharpness = 5.0
eps_norm = 1e-06
gelu_coef = 0.7978845608
cubic_coef = 0.044715

bf16 = jnp.bfloat16
f32 = jnp.float32
i32 = jnp.int32
MESH = pl.DeviceIdType.MESH


def coordinates():
    grp = lax.axis_index("grp")
    peak = lax.axis_index("peak")
    return (grp // 2) % 4, peak // 4, (peak % 4) * 2 + grp // 8, grp % 2


def device(x, y, z, core):
    return {"grp": ((z % 2) * 4 + x) * 2 + core, "peak": y * 4 + z // 2}


def rows_of(start, size):
    return pl.ds(pl.multiple_of(start, size), size)


STEPS = [(dx, dy) for dx in range(4) for dy in range(4) if dx or dy]


def gather_kernel(
    counts, tile_mask, neighbours, weight,
    hidden_out, turned_out, tallies_out,
    loaded, masked, turned, w_buf, mask_buf, own_lists, core_send, core_recv, plane_send,
    plane_recv, column, hidden, lists, list_rows, counted, tallies,
    load_sem, w_sem, core_ss, core_rs, plane_ss, plane_rs, z_ss, z_rs,
    out_ss, out_rs, fwd_ss, fwd_rs, list_ss, list_rs, store_sem,
):
    x, y, z, core = coordinates()
    plane = x * 4 + y

    def send(source, target, send_sem, recv_sem, to):
        return pltpu.make_async_remote_copy(
            src_ref=source, dst_ref=target, send_sem=send_sem, recv_sem=recv_sem,
            device_id=to, device_id_type=MESH,
        )

    sibling = device(x, y, z, 1 - core)
    plane_to = [((x + dx) % 4, (y + dy) % 4) for dx, dy in STEPS]
    plane_from = [((x + 4 - dx) % 4, (y + 4 - dy) % 4) for dx, dy in STEPS]
    plane_device = [device(px, py, z, core) for px, py in plane_to]
    column_device = [device(x, y, (z + step) % 8, core) for step in range(1, 8)]

    barrier = pltpu.get_barrier_semaphore()
    for other in [sibling] + plane_device + column_device:
        pl.semaphore_signal(barrier, inc=1, device_id=other, device_id_type=MESH)

    def block_start(step):
        return HALF * ((core + 1 + step) % 2) + BLOCK * (step // 2)

    def load(step):
        rows = rows_of(block_start(step), BLOCK)
        return pltpu.make_async_copy(counts.at[rows], loaded.at[rows], load_sem.at[step])

    w_copy = pltpu.make_async_copy(weight, w_buf, w_sem.at[0])
    mask_copy = pltpu.make_async_copy(tile_mask, mask_buf, w_sem.at[1])
    lists_copy = pltpu.make_async_copy(neighbours, own_lists, w_sem.at[2])
    mask_copy.start()
    load(0).start()
    w_copy.start()
    lists_copy.start()
    for step in range(1, 4):
        load(step).start()

    own_slot = (z * 16 + plane) * 2 + core

    def list_copies():
        return (
            [send(lists.at[own_slot], lists.at[own_slot], list_ss.at[0], list_rs.at[0], sibling)],
            [
                send(
                    lists.at[pl.ds((z * 16 + plane) * 2, 2)],
                    lists.at[pl.ds((z * 16 + plane) * 2, 2)],
                    list_ss.at[1 + i], list_rs.at[1 + i], to,
                )
                for i, to in enumerate(plane_device)
            ],
            [
                send(
                    lists.at[pl.ds(z * 32, 32)], lists.at[pl.ds(z * 32, 32)],
                    list_ss.at[16 + i], list_rs.at[16 + i], to,
                )
                for i, to in enumerate(column_device)
            ],
        )

    list_core, list_plane, list_column = list_copies()

    def core_copy(chunk):
        return send(
            core_send.at[chunk], core_recv.at[chunk], core_ss.at[chunk], core_rs.at[chunk], sibling
        )

    def plane_copies(chunk):
        return [
            send(
                plane_send.at[chunk, px * 4 + py], plane_recv.at[chunk, i],
                plane_ss.at[chunk, i], plane_rs.at[chunk, i], plane_device[i],
            )
            for i, (px, py) in enumerate(plane_to)
        ]

    def column_copies(chunk):
        return [
            send(
                column.at[chunk, z], column.at[chunk, z],
                z_ss.at[chunk, i], z_rs.at[chunk, i], to,
            )
            for i, to in enumerate(column_device)
        ]

    def piece_rows(chunk, of):
        return rows_of(core * HALF + chunk * BLOCK + of * PIECE, PIECE)

    def out_copies(chunk):
        rows = piece_rows(chunk, plane)
        return [
            send(hidden.at[rows], hidden.at[rows], out_ss.at[chunk, i], out_rs.at[chunk, i], to)
            for i, to in enumerate(plane_device)
        ]

    def fwd_copy(chunk, i):
        px, py = plane_from[i - 1] if i else (x, y)
        rows = piece_rows(chunk, px * 4 + py)
        return send(
            hidden.at[rows], hidden.at[rows], fwd_ss.at[chunk, i], fwd_rs.at[chunk, i], sibling
        )

    def peak_term(step):
        rows = rows_of(block_start(step), BLOCK)
        load(step).wait()
        keep = mask_buf[:, rows].astype(f32).T.astype(bf16)
        for tile in range(LOCAL // TILE):
            lanes = slice(tile * TILE, (tile + 1) * TILE)
            masked[rows, lanes] = loaded[rows, lanes] * jnp.broadcast_to(
                keep[:, tile : tile + 1], (BLOCK, TILE)
            )
        return jnp.dot(masked[rows, :], w_buf[...], preferred_element_type=f32)

    mask_copy.wait()
    w_copy.wait()

    def peak_chunk(chunk, carry):
        core_send[chunk] = peak_term(2 * chunk).astype(bf16)

        @pl.when(chunk == 0)
        def _():
            lists_copy.wait()
            lists[own_slot] = jnp.zeros((1, 128), i32)
            for cell in range(4):
                lists[own_slot, :, cell * SLOT : cell * SLOT + K] = own_lists[cell : cell + 1, :]
            pl.semaphore_wait(barrier, 23)
            for copy in list_core:
                copy.start()

        core_copy(chunk).start()
        term = peak_term(2 * chunk + 1)
        core_copy(chunk).wait()
        plane_send[chunk] = (term + core_recv[chunk].astype(f32)).astype(bf16).reshape(
            16, PIECE, D
        )
        for copy in plane_copies(chunk):
            copy.start()

        @pl.when(chunk == 0)
        def _():
            for copy in list_core:
                copy.wait()
            for copy in list_plane:
                copy.start()

        return carry

    lax.fori_loop(0, 2, peak_chunk, 0)
    for copy in list_plane:
        copy.wait()
    for copy in list_column:
        copy.start()

    def turn(step, carry):
        rows = rows_of(step * 128, 128)
        for tile in range(LOCAL // TILE):
            lanes = slice(tile * TILE, (tile + 1) * TILE)
            turned[lanes, rows] = masked[rows, lanes].T
        return carry

    def add_plane(chunk):
        total = plane_send[chunk, plane].astype(f32)
        for i, copy in enumerate(plane_copies(chunk)):
            copy.wait()
            total += plane_recv[chunk, i].astype(f32)
        column[chunk, z] = total.astype(bf16)
        for copy in column_copies(chunk):
            copy.start()

    lax.fori_loop(0, 4, turn, 0)
    add_plane(0)
    lax.fori_loop(4, 8, turn, 0)
    turned_store = pltpu.make_async_copy(turned, turned_out, store_sem.at[0])
    turned_store.start()
    add_plane(1)
    for copy in list_column:
        copy.wait()

    by_slot = lists[:, 0, :].astype(f32).T
    place = lax.broadcasted_iota(i32, (CELLS // 4, 1), 0)
    at_core, at_y, at_x, at_z = place % 2, (place // 2) % 4, (place // 8) % 4, place // 32
    holder = (((at_z % 2) * 4 + at_x) * 2 + at_core) * 16 + at_y * 4 + at_z // 2
    cells = lax.broadcasted_iota(i32, (CELLS // 4, CELLS), 1)
    gathered = jnp.zeros((2 * SLOT, CELLS), f32)
    for cell in range(4):
        chosen = (holder * 4 + cell == cells).astype(f32).astype(bf16)
        entry = by_slot[cell * SLOT : (cell + 1) * SLOT, :]
        high = jnp.floor(entry * (1.0 / 32.0))
        low = entry - 32.0 * high
        gathered += jnp.dot(
            jnp.concatenate([high, low], axis=0).astype(bf16), chosen, preferred_element_type=f32
        )
    list_rows[...] = gathered

    def count(part, carry):
        lanes = rows_of(part * 128, 128)
        ids = lax.broadcasted_iota(i32, (32, 128), 0).astype(f32)
        low_is, high = [], []
        for slot in range(K):
            entry = jnp.broadcast_to(list_rows[SLOT + slot : SLOT + slot + 1, lanes], (32, 128))
            low_is.append(jnp.where(entry == ids, 1.0, 0.0).astype(bf16))
            entry = jnp.broadcast_to(list_rows[slot : slot + 1, lanes], (32, 128))
            high.append(entry.astype(bf16))
        none = jnp.zeros((32, 128), bf16)

        def count_rows(step, carry):
            this = jnp.full((32, 128), step.astype(f32), f32).astype(bf16)
            total = none
            for slot in range(K):
                total += jnp.where(high[slot] == this, low_is[slot], none)
            counted[rows_of(step * 32, 32), lanes] = total
            return carry

        return lax.fori_loop(0, CELLS // 32, count_rows, carry, unroll=4)

    def add_column(chunk):
        for copy in column_copies(chunk):
            copy.wait()
        whole = column[chunk, 0].astype(f32)
        for step in range(1, 8):
            whole += column[chunk, step].astype(f32)
        hidden[piece_rows(chunk, plane), :] = whole.astype(bf16)
        for copy in out_copies(chunk):
            copy.start()
        fwd_copy(chunk, 0).start()

    def pass_on(chunk):
        for i, arrived in enumerate(out_copies(chunk)):
            arrived.wait()
            fwd_copy(chunk, i + 1).start()

    lax.fori_loop(0, 3, count, 0)
    add_column(0)
    lax.fori_loop(3, 8, count, 0)
    add_column(1)

    def both(step, carry):
        rows = rows_of(step * 128, 128)
        for part in range(CELLS // 128):
            lanes = slice(part * 128, (part + 1) * 128)
            tallies[rows, lanes] = counted[rows, lanes] + counted[lanes, rows].T
        return carry

    lax.fori_loop(0, CELLS // 128, both, 0)
    tallies_store = pltpu.make_async_copy(tallies, tallies_out, store_sem.at[1])
    tallies_store.start()
    pass_on(0)
    pass_on(1)
    for chunk in range(2):
        for i in range(16):
            fwd_copy(chunk, i).wait()
    hidden_store = pltpu.make_async_copy(hidden, hidden_out, store_sem.at[2])
    hidden_store.start()
    hidden_store.wait()
    turned_store.wait()
    tallies_store.wait()


MASK_T = True


def gather_hidden(counts, tile_mask, neighbours, weight):
    hbm = pl.BlockSpec(memory_space=pltpu.HBM)
    dma = pltpu.SemaphoreType.DMA
    return pl.pallas_call(
        gather_kernel,
        name="gather_hidden",
        out_shape=(
            jax.ShapeDtypeStruct((CELLS, D), bf16),
            jax.ShapeDtypeStruct((LOCAL, CELLS), bf16),
            jax.ShapeDtypeStruct((CELLS, CELLS), bf16),
        ),
        in_specs=[hbm, hbm, hbm, hbm],
        out_specs=(pl.BlockSpec(memory_space=pl.ANY), hbm, hbm),
        scratch_shapes=[
            pltpu.VMEM((CELLS, LOCAL), bf16),
            pltpu.VMEM((CELLS, LOCAL), bf16),
            pltpu.VMEM((LOCAL, CELLS), bf16),
            pltpu.VMEM((LOCAL, D), bf16),
            pltpu.VMEM((LOCAL // TILE, CELLS), i32),
            pltpu.VMEM((4, K), i32),
            pltpu.VMEM((2, BLOCK, D), bf16),
            pltpu.VMEM((2, BLOCK, D), bf16),
            pltpu.VMEM((2, 16, PIECE, D), bf16),
            pltpu.VMEM((2, 15, PIECE, D), bf16),
            pltpu.VMEM((2, 8, PIECE, D), bf16),
            pltpu.VMEM((CELLS, D), bf16),
            pltpu.VMEM((CELLS // 4, 1, 128), i32),
            pltpu.VMEM((2 * SLOT, CELLS), f32),
            pltpu.VMEM((CELLS, CELLS), bf16),
            pltpu.VMEM((CELLS, CELLS), bf16),
            dma((4,)), dma((3,)), dma((2,)), dma((2,)), dma((2, 15)), dma((2, 15)),
            dma((2, 7)), dma((2, 7)), dma((2, 15)), dma((2, 15)), dma((2, 16)), dma((2, 16)),
            dma((23,)), dma((23,)), dma((3,)),
        ],
        compiler_params=pltpu.CompilerParams(
            collective_id=0, has_side_effects=True, vmem_limit_bytes=48 << 20
        ),
        cost_estimate=pl.CostEstimate(
            flops=2 * CELLS * LOCAL * D, bytes_accessed=16 << 20, transcendentals=0
        ),
    )(*(pltpu.with_memory_space_constraint(v, pltpu.HBM) for v in (counts, tile_mask, neighbours, weight)))


def across(left, right):
    return lax.dot_general(left, right, (((1,), (1,)), ((), ())), preferred_element_type=f32)


def collapsed(left, right):
    return lax.dot_general(left, right, (((0,), (0,)), ((), ())), preferred_element_type=f32)


def tower_kernel(
    hidden, turned, tallies, gain, w_in, w_out,
    peak_grad, gain_grad, in_grad, out_grad,
    turned_buf, tallies_buf, rounded, slope, activ, unit, length, scale, codes, expo, inverse,
    dproj, dpre, dhidden, peak_buf, load_sem, store_sem,
):
    tallies_copy = pltpu.make_async_copy(tallies, tallies_buf, load_sem.at[0])
    tallies_copy.start()
    turned_copy = pltpu.make_async_copy(turned, turned_buf, load_sem.at[1])
    turned_copy.start()

    step_rows = 512
    steps = CELLS // step_rows

    def forward(step, carry):
        rows = rows_of(step * step_rows, step_rows)
        h = hidden[rows, :].astype(f32)
        s = lax.rsqrt(jnp.mean(h * h, axis=1, keepdims=True) + eps_norm)
        scale[rows, :] = s
        r = (h * s * gain[...]).astype(bf16)
        rounded[rows, :] = r
        v = jnp.dot(r, w_in[...], preferred_element_type=f32)
        t = jnp.tanh(gelu_coef * (v + cubic_coef * v * v * v))
        a = (0.5 * v * (1.0 + t)).astype(bf16)
        activ[rows, :] = a
        slope[rows, :] = 0.5 * (1.0 + t) + 0.5 * v * (1.0 - t * t) * gelu_coef * (
            1.0 + 3.0 * cubic_coef * v * v
        )
        p = jnp.dot(a, w_out[...], preferred_element_type=f32)
        n = lax.rsqrt(jnp.sum(p * p, axis=1, keepdims=True) + eps_norm)
        length[rows, :] = n
        u = p * n
        unit[rows, :] = u
        codes[rows, :] = u.astype(bf16)
        return carry

    lax.fori_loop(0, steps, forward, 0)

    def score(step, column_total):
        rows = rows_of(step * step_rows, step_rows)
        e = jnp.exp(across(codes[rows, :], codes[...]) * sharpness)
        own = lax.broadcasted_iota(i32, (step_rows, CELLS), 0) + step * step_rows
        other = lax.broadcasted_iota(i32, (step_rows, CELLS), 1)
        e = jnp.where(own == other, 0.0, e)
        expo[rows, :] = e
        inverse[rows, :] = 1.0 / jnp.sum(e, axis=1, keepdims=True)
        return column_total + jnp.sum(e, axis=0, keepdims=True)

    column_inverse = 1.0 / lax.fori_loop(0, steps, score, jnp.zeros((1, CELLS), f32))
    tallies_copy.wait()

    def backward(step, gain_total):
        rows = rows_of(step * step_rows, step_rows)
        both = expo[rows, :] * (inverse[rows, :] + column_inverse)
        both = (both - tallies_buf[rows, :].astype(f32) * (1.0 / K)).astype(bf16)
        dcodes = jnp.dot(both, codes[...], preferred_element_type=f32) * sharpness
        u = unit[rows, :]
        dp = (length[rows, :] * (dcodes - u * jnp.sum(u * dcodes, axis=1, keepdims=True))).astype(bf16)
        dproj[rows, :] = dp
        dv = (across(dp, w_out[...]) * slope[rows, :]).astype(bf16)
        dpre[rows, :] = dv
        dround = across(dv, w_in[...])
        s = scale[rows, :]
        normed = hidden[rows, :].astype(f32) * s
        dnorm = dround * gain[...]
        dhidden[rows, :] = (
            s * (dnorm - normed * jnp.mean(dnorm * normed, axis=1, keepdims=True))
        ).astype(bf16)
        return gain_total + jnp.sum(dround * normed, axis=0, keepdims=True)

    gain_grad[...] = lax.fori_loop(0, steps, backward, jnp.zeros((1, D), f32))
    turned_copy.wait()

    def store(step):
        rows = rows_of(step * step_rows, step_rows)
        return pltpu.make_async_copy(peak_buf.at[rows], peak_grad.at[rows], store_sem.at[step])

    def peak(step, carry):
        rows = rows_of(step * step_rows, step_rows)
        peak_buf[rows, :] = jnp.dot(turned_buf[rows, :], dhidden[...], preferred_element_type=f32)
        store(step).start()
        return carry

    lax.fori_loop(0, LOCAL // step_rows, peak, 0)
    in_grad[...] = collapsed(rounded[...], dpre[...])
    out_grad[...] = collapsed(activ[...], dproj[...])

    def stored(step, carry):
        store(step).wait()
        return carry

    lax.fori_loop(0, LOCAL // step_rows, stored, 0)


def tower(hidden, turned, tallies, gain, w_in, w_out):
    any_space = pl.BlockSpec(memory_space=pl.ANY)
    vmem = pl.BlockSpec(memory_space=pltpu.VMEM)
    dma = pltpu.SemaphoreType.DMA
    return pl.pallas_call(
        tower_kernel,
        name="tower",
        out_shape=(
            jax.ShapeDtypeStruct((LOCAL, D), f32),
            jax.ShapeDtypeStruct((1, D), f32),
            jax.ShapeDtypeStruct((D, HID), f32),
            jax.ShapeDtypeStruct((HID, E), f32),
        ),
        in_specs=[vmem, any_space, any_space, vmem, vmem, vmem],
        out_specs=(any_space, vmem, vmem, vmem),
        scratch_shapes=[
            pltpu.VMEM((LOCAL, CELLS), bf16),
            pltpu.VMEM((CELLS, CELLS), bf16),
            pltpu.VMEM((CELLS, D), bf16),
            pltpu.VMEM((CELLS, HID), f32),
            pltpu.VMEM((CELLS, HID), bf16),
            pltpu.VMEM((CELLS, E), f32),
            pltpu.VMEM((CELLS, 1), f32),
            pltpu.VMEM((CELLS, 1), f32),
            pltpu.VMEM((CELLS, E), bf16),
            pltpu.VMEM((CELLS, CELLS), f32),
            pltpu.VMEM((CELLS, 1), f32),
            pltpu.VMEM((CELLS, E), bf16),
            pltpu.VMEM((CELLS, HID), bf16),
            pltpu.VMEM((CELLS, D), bf16),
            pltpu.VMEM((LOCAL, D), f32),
            dma((2,)), dma((8,)),
        ],
        compiler_params=pltpu.CompilerParams(vmem_limit_bytes=46 << 20),
        cost_estimate=pl.CostEstimate(
            flops=6 << 30, bytes_accessed=16 << 20, transcendentals=2 << 20
        ),
    )(hidden, turned, tallies, gain, w_in, w_out)


def body(counts, tile_mask, neighbours, peak_weight, gain, w_in, w_out):
    hidden, turned, tallies = gather_hidden(counts, tile_mask.T, neighbours, peak_weight)
    turned = pltpu.with_memory_space_constraint(turned, pltpu.HBM)
    peak_grad, gain_grad, in_grad, out_grad = tower(
        hidden, turned, tallies, gain.reshape(1, D), w_in, w_out
    )
    return (peak_grad, gain_grad.reshape(D), in_grad, out_grad)


def solution(mesh):
    cells = P(("grp", "peak"), None)
    peaks = P(None, ("grp", "peak"))
    return jax.shard_map(
        body,
        mesh=mesh,
        in_specs=(peaks, peaks, cells, cells, P(), P(), P()),
        out_specs=(cells, P(), P(), P()),
        check_vma=False,
    )
```

time: 64.1 us -> 55.6 us (0.87)
  Pallas kernels: 59.8 us -> 54.8 us
  local copies, waits for them, and re-layouts: 3.37 us -> 0.01 us
    unnamed x11 -> x6, local copies, waits for them, and re-layouts: 3.37 us -> 0.01 us
    pallas_call x1, Pallas kernels: 15.3 us -> 12.3 us  [tower(): pl.pallas_call(tower_kernel, name='tower', out_shape=(jax.ShapeDtypeStruc...]
    pallas_call x1, Pallas kernels: 44.5 us -> 42.4 us  [gather_hidden(): pl.pallas_call(gather_kernel, name='gather_hidden', out_shape=(jax.ShapeD...]
where the time goes in v2:
time: 55.6 us; the launch traced here: 55.5 us
  Pallas kernels  54.8 us (99%)
  between operations  0.69 us (1%)
    pallas_call x1, Pallas kernels, gather_hidden(): pl.pallas_call(gather_kernel, name='gather_hidden', out_shape=(jax.ShapeD...  42.4 us
    pallas_call x1, Pallas kernels, tower(): pl.pallas_call(tower_kernel, name='tower', out_shape=(jax.ShapeDtypeStruc...  12.3 us

profile of v2, /device:TPU:1, one launch (start us, length us, event | category | flops | bytes accessed | tf_op | source)
XLA Modules:
  0.0 55.5 jit_solution(6178423097628179571)
XLA Ops:
  0.6 0.0 copy-start.1
  0.6 0.0 copy-start
  0.7 0.0 copy-start.2
  0.7 42.4 %gather_hidden.1 = (bf16[1024,512]{1,0:T(8,128)(2,1)S(1)}, bf16[2048,1024]{1,0:T(8,128)(2,1)}, bf16[1024,1024]{1,0:T(8,128)(2,1)S(1)}) custom-call(bf16[1024,2048]{1,0:T(8,128)(2,1)} %counts.1, s32[16,1024]{1,0:T(8,128)} %bitcast.4, s32[4,15]{1,0:T(4,128)} %neighbours.1, bf16[2048,512]{1,0:T(8,128)(2,1)} %weight.1), custom_call_target="tpu_custom_call" | custom-call | flops 2147483648 | bytes 16777216 | tf_op jit(solution)/shard_map/gather_hidden/pallas_call | solution.py:318
  43.1 0.0 copy-done.1
  43.1 0.0 copy-done
  43.1 0.0 copy-done.2
  43.1 12.3 %tower.1 = (f32[2048,512]{1,0:T(8,128)}, f32[1,512]{1,0:T(1,128)}, f32[512,512]{1,0:T(8,128)}, f32[512,256]{1,0:T(8,128)}) custom-call(bf16[1024,512]{1,0:T(8,128)(2,1)S(1)} %get-tuple-element.11.hidden, bf16[2048,1024]{1,0:T(8,128)(2,1)} %get-tuple-element.12.turned, bf16[1024,1024]{1,0:T(8,128)(2,1)S(1)} %get-tuple-element.13.tallies, ...), custom_call_target="tpu_custom_call" | custom-call | flops 6442450944 | bytes 16777216 | tf_op jit(solution)/shard_map/tower/pallas_call | solution.py:464
Async XLA Ops:
  0.6 42.5 %copy-start.1 = (bf16[512,256]{1,0:T(8,128)(2,1)S(1)}, bf16[512,256]{1,0:T(8,128)(2,1)}, u32[]{:S(2)}) copy-start(bf16[512,256]{1,0:T(8,128)(2,1)} %w_out.1) | copy-start | bytes 786436
  0.6 42.5 %copy-start = (bf16[512,512]{1,0:T(8,128)(2,1)S(1)}, bf16[512,512]{1,0:T(8,128)(2,1)}, u32[]{:S(2)}) copy-start(bf16[512,512]{1,0:T(8,128)(2,1)} %w_in.1) | copy-start | bytes 1572868
  0.7 42.5 %copy-start.2 = (f32[512]{0:T(512)S(1)}, f32[512]{0:T(512)}, u32[]{:S(2)}) copy-start(f32[512]{0:T(512)} %param.11) | copy-start | bytes 6148

commit v3 on v2

--- a/solution.py
+++ b/solution.py
@@ -89,29 +89,19 @@
     for step in range(1, 4):
         load(step).start()
 
-    own_slot = (z * 16 + plane) * 2 + core
-
-    def list_copies():
-        return (
-            [send(lists.at[own_slot], lists.at[own_slot], list_ss.at[0], list_rs.at[0], sibling)],
-            [
-                send(
-                    lists.at[pl.ds((z * 16 + plane) * 2, 2)],
-                    lists.at[pl.ds((z * 16 + plane) * 2, 2)],
-                    list_ss.at[1 + i], list_rs.at[1 + i], to,
-                )
-                for i, to in enumerate(plane_device)
-            ],
-            [
-                send(
-                    lists.at[pl.ds(z * 32, 32)], lists.at[pl.ds(z * 32, 32)],
-                    list_ss.at[16 + i], list_rs.at[16 + i], to,
-                )
-                for i, to in enumerate(column_device)
-            ],
-        )
-
-    list_core, list_plane, list_column = list_copies()
+    own_slot = core * 128 + z * 16 + plane
+
+    list_plane = [
+        send(lists.at[own_slot], lists.at[own_slot], list_ss.at[i], list_rs.at[i], to)
+        for i, to in enumerate(plane_device)
+    ]
+    list_layer = lists.at[pl.ds(core * 128 + z * 16, 16)]
+    list_column = [
+        send(list_layer, list_layer, list_ss.at[15 + i], list_rs.at[15 + i], to)
+        for i, to in enumerate(column_device)
+    ]
+    list_half = lists.at[pl.ds(core * 128, 128)]
+    list_core = send(list_half, list_half, list_ss.at[22], list_rs.at[22], sibling)
 
     def core_copy(chunk):
         return send(
@@ -177,10 +167,14 @@
             for cell in range(4):
                 lists[own_slot, :, cell * SLOT : cell * SLOT + K] = own_lists[cell : cell + 1, :]
             pl.semaphore_wait(barrier, 23)
-            for copy in list_core:
+
+        core_copy(chunk).start()
+
+        @pl.when(chunk == 0)
+        def _():
+            for copy in list_plane:
                 copy.start()
 
-        core_copy(chunk).start()
         term = peak_term(2 * chunk + 1)
         core_copy(chunk).wait()
         plane_send[chunk] = (term + core_recv[chunk].astype(f32)).astype(bf16).reshape(
@@ -188,14 +182,6 @@
         )
         for copy in plane_copies(chunk):
             copy.start()
-
-        @pl.when(chunk == 0)
-        def _():
-            for copy in list_core:
-                copy.wait()
-            for copy in list_plane:
-                copy.start()
-
         return carry
 
     lax.fori_loop(0, 2, peak_chunk, 0)
@@ -220,18 +206,21 @@
         for copy in column_copies(chunk):
             copy.start()
 
-    lax.fori_loop(0, 4, turn, 0)
+    lax.fori_loop(0, 3, turn, 0)
     add_plane(0)
-    lax.fori_loop(4, 8, turn, 0)
-    turned_store = pltpu.make_async_copy(turned, turned_out, store_sem.at[0])
-    turned_store.start()
+    lax.fori_loop(3, 6, turn, 0)
     add_plane(1)
     for copy in list_column:
         copy.wait()
+    list_core.start()
+    lax.fori_loop(6, 8, turn, 0)
+    turned_store = pltpu.make_async_copy(turned, turned_out, store_sem.at[0])
+    turned_store.start()
+    list_core.wait()
 
     by_slot = lists[:, 0, :].astype(f32).T
     place = lax.broadcasted_iota(i32, (CELLS // 4, 1), 0)
-    at_core, at_y, at_x, at_z = place % 2, (place // 2) % 4, (place // 8) % 4, place // 32
+    at_core, at_z, at_x, at_y = place // 128, (place // 16) % 8, (place // 4) % 4, place % 4
     holder = (((at_z % 2) * 4 + at_x) * 2 + at_core) * 16 + at_y * 4 + at_z // 2
     cells = lax.broadcasted_iota(i32, (CELLS // 4, CELLS), 1)
     gathered = jnp.zeros((2 * SLOT, CELLS), f32)
@@ -299,12 +288,20 @@
     tallies_store.start()
     pass_on(0)
     pass_on(1)
+    hidden_stores = []
     for chunk in range(2):
         for i in range(16):
             fwd_copy(chunk, i).wait()
-    hidden_store = pltpu.make_async_copy(hidden, hidden_out, store_sem.at[2])
-    hidden_store.start()
-    hidden_store.wait()
+        for half in range(2):
+            rows = pl.ds(half * HALF + chunk * BLOCK, BLOCK)
+            hidden_stores.append(
+                pltpu.make_async_copy(
+                    hidden.at[rows], hidden_out.at[rows], store_sem.at[2 + 2 * chunk + half]
+                )
+            )
+            hidden_stores[-1].start()
+    for copy in hidden_stores:
+        copy.wait()
     turned_store.wait()
     tallies_store.wait()
 
@@ -344,7 +341,7 @@
             pltpu.VMEM((CELLS, CELLS), bf16),
             dma((4,)), dma((3,)), dma((2,)), dma((2,)), dma((2, 15)), dma((2, 15)),
             dma((2, 7)), dma((2, 7)), dma((2, 15)), dma((2, 15)), dma((2, 16)), dma((2, 16)),
-            dma((23,)), dma((23,)), dma((3,)),
+            dma((23,)), dma((23,)), dma((6,)),
         ],
         compiler_params=pltpu.CompilerParams(
             collective_id=0, has_side_effects=True, vmem_limit_bytes=48 << 20
@@ -367,7 +364,7 @@
     hidden, turned, tallies, gain, w_in, w_out,
     peak_grad, gain_grad, in_grad, out_grad,
     turned_buf, tallies_buf, rounded, slope, activ, unit, length, scale, codes, expo, inverse,
-    dproj, dpre, dhidden, peak_buf, load_sem, store_sem,
+    dproj, dpre, dhidden, peak_buf, in_buf, out_buf, load_sem, store_sem,
 ):
     tallies_copy = pltpu.make_async_copy(tallies, tallies_buf, load_sem.at[0])
     tallies_copy.start()
@@ -375,7 +372,6 @@
     turned_copy.start()
 
     step_rows = 512
-    steps = CELLS // step_rows
 
     def forward(step, carry):
         rows = rows_of(step * step_rows, step_rows)
@@ -399,41 +395,39 @@
         codes[rows, :] = u.astype(bf16)
         return carry
 
-    lax.fori_loop(0, steps, forward, 0)
-
-    def score(step, column_total):
-        rows = rows_of(step * step_rows, step_rows)
-        e = jnp.exp(across(codes[rows, :], codes[...]) * sharpness)
-        own = lax.broadcasted_iota(i32, (step_rows, CELLS), 0) + step * step_rows
-        other = lax.broadcasted_iota(i32, (step_rows, CELLS), 1)
-        e = jnp.where(own == other, 0.0, e)
-        expo[rows, :] = e
-        inverse[rows, :] = 1.0 / jnp.sum(e, axis=1, keepdims=True)
-        return column_total + jnp.sum(e, axis=0, keepdims=True)
-
-    column_inverse = 1.0 / lax.fori_loop(0, steps, score, jnp.zeros((1, CELLS), f32))
+    lax.fori_loop(0, CELLS // step_rows, forward, 0)
+
+    e = jnp.exp(across(codes[...], codes[...]) * sharpness)
+    own = lax.broadcasted_iota(i32, (CELLS, CELLS), 0)
+    other = lax.broadcasted_iota(i32, (CELLS, CELLS), 1)
+    e = jnp.where(own == other, 0.0, e)
+    expo[...] = e
+    inverse[...] = 1.0 / jnp.sum(e, axis=1, keepdims=True)
+    column_inverse = 1.0 / jnp.sum(e, axis=0, keepdims=True)
     tallies_copy.wait()
 
-    def backward(step, gain_total):
-        rows = rows_of(step * step_rows, step_rows)
-        both = expo[rows, :] * (inverse[rows, :] + column_inverse)
-        both = (both - tallies_buf[rows, :].astype(f32) * (1.0 / K)).astype(bf16)
-        dcodes = jnp.dot(both, codes[...], preferred_element_type=f32) * sharpness
-        u = unit[rows, :]
-        dp = (length[rows, :] * (dcodes - u * jnp.sum(u * dcodes, axis=1, keepdims=True))).astype(bf16)
-        dproj[rows, :] = dp
-        dv = (across(dp, w_out[...]) * slope[rows, :]).astype(bf16)
-        dpre[rows, :] = dv
-        dround = across(dv, w_in[...])
-        s = scale[rows, :]
-        normed = hidden[rows, :].astype(f32) * s
-        dnorm = dround * gain[...]
-        dhidden[rows, :] = (
-            s * (dnorm - normed * jnp.mean(dnorm * normed, axis=1, keepdims=True))
-        ).astype(bf16)
-        return gain_total + jnp.sum(dround * normed, axis=0, keepdims=True)
-
-    gain_grad[...] = lax.fori_loop(0, steps, backward, jnp.zeros((1, D), f32))
+    both = expo[...] * (inverse[...] + column_inverse)
+    both = (both - tallies_buf[...].astype(f32) * (1.0 / K)).astype(bf16)
+    dcodes = jnp.dot(both, codes[...], preferred_element_type=f32) * sharpness
+    u = unit[...]
+    dp = (length[...] * (dcodes - u * jnp.sum(u * dcodes, axis=1, keepdims=True))).astype(bf16)
+    dproj[...] = dp
+    dv = (across(dp, w_out[...]) * slope[...]).astype(bf16)
+    dpre[...] = dv
+    dround = across(dv, w_in[...])
+    normed = hidden[...].astype(f32) * scale[...]
+    dnorm = dround * gain[...]
+    dhidden[...] = (
+        scale[...] * (dnorm - normed * jnp.mean(dnorm * normed, axis=1, keepdims=True))
+    ).astype(bf16)
+    gain_grad[...] = jnp.sum(dround * normed, axis=0, keepdims=True)
+
+    in_buf[...] = collapsed(rounded[...], dpre[...])
+    in_store = pltpu.make_async_copy(in_buf, in_grad, store_sem.at[4])
+    in_store.start()
+    out_buf[...] = collapsed(activ[...], dproj[...])
+    out_store = pltpu.make_async_copy(out_buf, out_grad, store_sem.at[5])
+    out_store.start()
     turned_copy.wait()
 
     def store(step):
@@ -447,9 +441,8 @@
         return carry
 
     lax.fori_loop(0, LOCAL // step_rows, peak, 0)
-    in_grad[...] = collapsed(rounded[...], dpre[...])
-    out_grad[...] = collapsed(activ[...], dproj[...])
-
+    in_store.wait()
+    out_store.wait()
     def stored(step, carry):
         store(step).wait()
         return carry
@@ -471,7 +464,7 @@
             jax.ShapeDtypeStruct((HID, E), f32),
         ),
         in_specs=[vmem, any_space, any_space, vmem, vmem, vmem],
-        out_specs=(any_space, vmem, vmem, vmem),
+        out_specs=(any_space, vmem, any_space, any_space),
         scratch_shapes=[
             pltpu.VMEM((LOCAL, CELLS), bf16),
             pltpu.VMEM((CELLS, CELLS), bf16),
@@ -488,7 +481,9 @@
             pltpu.VMEM((CELLS, HID), bf16),
             pltpu.VMEM((CELLS, D), bf16),
             pltpu.VMEM((LOCAL, D), f32),
-            dma((2,)), dma((8,)),
+            pltpu.VMEM((D, HID), f32),
+            pltpu.VMEM((HID, E), f32),
+            dma((2,)), dma((6,)),
         ],
         compiler_params=pltpu.CompilerParams(vmem_limit_bytes=46 << 20),
         cost_estimate=pl.CostEstimate(

time: 55.6 us -> 51.6 us (0.928)
  Pallas kernels: 54.8 us -> 50.8 us
    pallas_call x1, Pallas kernels: 42.4 us -> 39.1 us  [gather_hidden(): pl.pallas_call(gather_kernel, name='gather_hidden', out_shape=(jax.ShapeD...]
    pallas_call x1, Pallas kernels: 12.3 us -> 11.7 us  [tower(): pl.pallas_call(tower_kernel, name='tower', out_shape=(jax.ShapeDtypeStruc...]
where the time goes in v3:
time: 51.6 us; the launch traced here: 51.5 us
  Pallas kernels  50.8 us (98%)
  between operations  0.69 us (1%)
    pallas_call x1, Pallas kernels, gather_hidden(): pl.pallas_call(gather_kernel, name='gather_hidden', out_shape=(jax.ShapeD...  39.1 us
    pallas_call x1, Pallas kernels, tower(): pl.pallas_call(tower_kernel, name='tower', out_shape=(jax.ShapeDtypeStruc...  11.7 us

profile of v3, /device:TPU:1, one launch (start us, length us, event | category | flops | bytes accessed | tf_op | source)
XLA Modules:
  0.0 51.5 jit_solution(1263116377056763793)
XLA Ops:
  0.6 0.0 copy-start.1
  0.6 0.0 copy-start
  0.7 0.0 copy-start.2
  0.7 39.1 %gather_hidden.1 = (bf16[1024,512]{1,0:T(8,128)(2,1)S(1)}, bf16[2048,1024]{1,0:T(8,128)(2,1)}, bf16[1024,1024]{1,0:T(8,128)(2,1)S(1)}) custom-call(bf16[1024,2048]{1,0:T(8,128)(2,1)} %counts.1, s32[16,1024]{1,0:T(8,128)} %bitcast.4, s32[4,15]{1,0:T(4,128)} %neighbours.1, bf16[2048,512]{1,0:T(8,128)(2,1)} %weight.1), custom_call_target="tpu_custom_call" | custom-call | flops 2147483648 | bytes 16777216 | tf_op jit(solution)/shard_map/gather_hidden/pallas_call | solution.py:315
  39.8 0.0 copy-done.1
  39.8 0.0 copy-done
  39.8 0.0 copy-done.2
  39.8 11.7 %tower.1 = (f32[2048,512]{1,0:T(8,128)}, f32[1,512]{1,0:T(1,128)}, f32[512,512]{1,0:T(8,128)}, f32[512,256]{1,0:T(8,128)}) custom-call(bf16[1024,512]{1,0:T(8,128)(2,1)S(1)} %get-tuple-element.11.hidden, bf16[2048,1024]{1,0:T(8,128)(2,1)} %get-tuple-element.12.turned, bf16[1024,1024]{1,0:T(8,128)(2,1)S(1)} %get-tuple-element.13.tallies, ...), custom_call_target="tpu_custom_call" | custom-call | flops 6442450944 | bytes 16777216 | tf_op jit(solution)/shard_map/tower/pallas_call | solution.py:457
Async XLA Ops:
  0.6 39.2 %copy-start.1 = (bf16[512,256]{1,0:T(8,128)(2,1)S(1)}, bf16[512,256]{1,0:T(8,128)(2,1)}, u32[]{:S(2)}) copy-start(bf16[512,256]{1,0:T(8,128)(2,1)} %w_out.1) | copy-start | bytes 786436
  0.6 39.2 %copy-start = (bf16[512,512]{1,0:T(8,128)(2,1)S(1)}, bf16[512,512]{1,0:T(8,128)(2,1)}, u32[]{:S(2)}) copy-start(bf16[512,512]{1,0:T(8,128)(2,1)} %w_in.1) | copy-start | bytes 1572868
  0.7 39.2 %copy-start.2 = (f32[512]{0:T(512)S(1)}, f32[512]{0:T(512)}, u32[]{:S(2)}) copy-start(f32[512]{0:T(512)} %param.11) | copy-start | bytes 6148

commit v4 on v3

--- a/solution.py
+++ b/solution.py
@@ -21,6 +21,7 @@
 eps_norm = 1e-06
 gelu_coef = 0.7978845608
 cubic_coef = 0.044715
+log2_e = 1.4426950408889634
 
 bf16 = jnp.bfloat16
 f32 = jnp.float32
@@ -49,7 +50,7 @@
     counts, tile_mask, neighbours, weight,
     hidden_out, turned_out, tallies_out,
     loaded, masked, turned, w_buf, mask_buf, own_lists, core_send, core_recv, plane_send,
-    plane_recv, column, hidden, lists, list_rows, counted, tallies,
+    plane_recv, column, own_piece, lists, list_rows, counted, tallies,
     load_sem, w_sem, core_ss, core_rs, plane_ss, plane_rs, z_ss, z_rs,
     out_ss, out_rs, fwd_ss, fwd_rs, list_ss, list_rs, store_sem,
 ):
@@ -64,7 +65,6 @@
 
     sibling = device(x, y, z, 1 - core)
     plane_to = [((x + dx) % 4, (y + dy) % 4) for dx, dy in STEPS]
-    plane_from = [((x + 4 - dx) % 4, (y + 4 - dy) % 4) for dx, dy in STEPS]
     plane_device = [device(px, py, z, core) for px, py in plane_to]
     column_device = [device(x, y, (z + step) % 8, core) for step in range(1, 8)]
 
@@ -129,18 +129,27 @@
     def piece_rows(chunk, of):
         return rows_of(core * HALF + chunk * BLOCK + of * PIECE, PIECE)
 
+    def keep_piece(chunk):
+        return pltpu.make_async_copy(
+            own_piece.at[chunk], hidden_out.at[piece_rows(chunk, plane)], store_sem.at[2 + chunk]
+        )
+
     def out_copies(chunk):
         rows = piece_rows(chunk, plane)
         return [
-            send(hidden.at[rows], hidden.at[rows], out_ss.at[chunk, i], out_rs.at[chunk, i], to)
+            send(
+                own_piece.at[chunk], hidden_out.at[rows],
+                out_ss.at[chunk, i], out_rs.at[chunk, i], to,
+            )
             for i, to in enumerate(plane_device)
         ]
 
-    def fwd_copy(chunk, i):
-        px, py = plane_from[i - 1] if i else (x, y)
-        rows = piece_rows(chunk, px * 4 + py)
+    def fwd_copy(chunk, dx):
+        start = core * HALF + chunk * BLOCK + ((x + 4 - dx) % 4) * 4 * PIECE
+        rows = rows_of(start, 4 * PIECE)
         return send(
-            hidden.at[rows], hidden.at[rows], fwd_ss.at[chunk, i], fwd_rs.at[chunk, i], sibling
+            hidden_out.at[rows], hidden_out.at[rows],
+            fwd_ss.at[chunk, dx], fwd_rs.at[chunk, dx], sibling,
         )
 
     def peak_term(step):
@@ -200,7 +209,7 @@
     def add_plane(chunk):
         total = plane_send[chunk, plane].astype(f32)
         for i, copy in enumerate(plane_copies(chunk)):
-            copy.wait()
+            copy.wait_recv()
             total += plane_recv[chunk, i].astype(f32)
         column[chunk, z] = total.astype(bf16)
         for copy in column_copies(chunk):
@@ -257,19 +266,23 @@
 
     def add_column(chunk):
         for copy in column_copies(chunk):
-            copy.wait()
+            copy.wait_recv()
         whole = column[chunk, 0].astype(f32)
         for step in range(1, 8):
             whole += column[chunk, step].astype(f32)
-        hidden[piece_rows(chunk, plane), :] = whole.astype(bf16)
+        own_piece[chunk] = whole.astype(bf16)
         for copy in out_copies(chunk):
             copy.start()
-        fwd_copy(chunk, 0).start()
+        keep_piece(chunk).start()
 
     def pass_on(chunk):
-        for i, arrived in enumerate(out_copies(chunk)):
-            arrived.wait()
-            fwd_copy(chunk, i + 1).start()
+        arrived = out_copies(chunk)
+        keep_piece(chunk).wait()
+        for dx in range(4):
+            for i, step in enumerate(STEPS):
+                if step[0] == dx:
+                    arrived[i].wait_recv()
+            fwd_copy(chunk, dx).start()
 
     lax.fori_loop(0, 3, count, 0)
     add_column(0)
@@ -288,20 +301,12 @@
     tallies_store.start()
     pass_on(0)
     pass_on(1)
-    hidden_stores = []
     for chunk in range(2):
-        for i in range(16):
-            fwd_copy(chunk, i).wait()
-        for half in range(2):
-            rows = pl.ds(half * HALF + chunk * BLOCK, BLOCK)
-            hidden_stores.append(
-                pltpu.make_async_copy(
-                    hidden.at[rows], hidden_out.at[rows], store_sem.at[2 + 2 * chunk + half]
-                )
-            )
-            hidden_stores[-1].start()
-    for copy in hidden_stores:
-        copy.wait()
+        for copy in plane_copies(chunk) + column_copies(chunk) + out_copies(chunk):
+            copy.wait_send()
+    for chunk in range(2):
+        for dx in range(4):
+            fwd_copy(chunk, dx).wait()
     turned_store.wait()
     tallies_store.wait()
 
@@ -334,14 +339,14 @@
             pltpu.VMEM((2, 16, PIECE, D), bf16),
             pltpu.VMEM((2, 15, PIECE, D), bf16),
             pltpu.VMEM((2, 8, PIECE, D), bf16),
-            pltpu.VMEM((CELLS, D), bf16),
+            pltpu.VMEM((2, PIECE, D), bf16),
             pltpu.VMEM((CELLS // 4, 1, 128), i32),
             pltpu.VMEM((2 * SLOT, CELLS), f32),
             pltpu.VMEM((CELLS, CELLS), bf16),
             pltpu.VMEM((CELLS, CELLS), bf16),
             dma((4,)), dma((3,)), dma((2,)), dma((2,)), dma((2, 15)), dma((2, 15)),
-            dma((2, 7)), dma((2, 7)), dma((2, 15)), dma((2, 15)), dma((2, 16)), dma((2, 16)),
-            dma((23,)), dma((23,)), dma((6,)),
+            dma((2, 7)), dma((2, 7)), dma((2, 15)), dma((2, 15)), dma((2, 4)), dma((2, 4)),
+            dma((23,)), dma((23,)), dma((4,)),
         ],
         compiler_params=pltpu.CompilerParams(
             collective_id=0, has_side_effects=True, vmem_limit_bytes=48 << 20
@@ -381,11 +386,13 @@
         r = (h * s * gain[...]).astype(bf16)
         rounded[rows, :] = r
         v = jnp.dot(r, w_in[...], preferred_element_type=f32)
-        t = jnp.tanh(gelu_coef * (v + cubic_coef * v * v * v))
-        a = (0.5 * v * (1.0 + t)).astype(bf16)
+        square = v * v
+        t = jnp.tanh(v * (gelu_coef + (gelu_coef * cubic_coef) * square))
+        half_v = 0.5 * v
+        a = (half_v + half_v * t).astype(bf16)
         activ[rows, :] = a
-        slope[rows, :] = 0.5 * (1.0 + t) + 0.5 * v * (1.0 - t * t) * gelu_coef * (
-            1.0 + 3.0 * cubic_coef * v * v
+        slope[rows, :] = (0.5 + 0.5 * t) + half_v * (1.0 - t * t) * (
+            gelu_coef + (3.0 * gelu_coef * cubic_coef) * square
         )
         p = jnp.dot(a, w_out[...], preferred_element_type=f32)
         n = lax.rsqrt(jnp.sum(p * p, axis=1, keepdims=True) + eps_norm)
@@ -397,11 +404,12 @@
 
     lax.fori_loop(0, CELLS // step_rows, forward, 0)
 
-    e = jnp.exp(across(codes[...], codes[...]) * sharpness)
-    own = lax.broadcasted_iota(i32, (CELLS, CELLS), 0)
-    other = lax.broadcasted_iota(i32, (CELLS, CELLS), 1)
-    e = jnp.where(own == other, 0.0, e)
-    expo[...] = e
+    expo[...] = jnp.exp2(across(codes[...], codes[...]) * (sharpness * log2_e))
+    diagonal = lax.broadcasted_iota(i32, (128, 128), 0) == lax.broadcasted_iota(i32, (128, 128), 1)
+    for part in range(CELLS // 128):
+        block = slice(part * 128, (part + 1) * 128)
+        expo[block, block] = jnp.where(diagonal, 0.0, expo[block, block])
+    e = expo[...]
     inverse[...] = 1.0 / jnp.sum(e, axis=1, keepdims=True)
     column_inverse = 1.0 / jnp.sum(e, axis=0, keepdims=True)
     tallies_copy.wait()

time: 51.6 us -> 50.9 us (0.986)
  Pallas kernels: 50.8 us -> 50.1 us
where the time goes in v4:
time: 50.9 us; the launch traced here: 50.8 us
  Pallas kernels  50.1 us (98%)
  between operations  0.69 us (1%)
    pallas_call x1, Pallas kernels, gather_hidden(): pl.pallas_call(gather_kernel, name='gather_hidden', out_shape=(jax.ShapeD...  38.6 us
    pallas_call x1, Pallas kernels, tower(): pl.pallas_call(tower_kernel, name='tower', out_shape=(jax.ShapeDtypeStruc...  11.5 us

profile of v4, /device:TPU:1, one launch (start us, length us, event | category | flops | bytes accessed | tf_op | source)
XLA Modules:
  0.0 50.8 jit_solution(14495115870772017640)
XLA Ops:
  0.6 0.0 copy-start.1
  0.6 0.0 copy-start
  0.7 0.0 copy-start.2
  0.7 38.6 %gather_hidden.1 = (bf16[1024,512]{1,0:T(8,128)(2,1)S(1)}, bf16[2048,1024]{1,0:T(8,128)(2,1)}, bf16[1024,1024]{1,0:T(8,128)(2,1)S(1)}) custom-call(bf16[1024,2048]{1,0:T(8,128)(2,1)} %counts.1, s32[16,1024]{1,0:T(8,128)} %bitcast.4, s32[4,15]{1,0:T(4,128)} %neighbours.1, bf16[2048,512]{1,0:T(8,128)(2,1)} %weight.1), custom_call_target="tpu_custom_call" | custom-call | flops 2147483648 | bytes 16777216 | tf_op jit(solution)/shard_map/gather_hidden/pallas_call | solution.py:320
  39.3 0.0 copy-done.1
  39.3 0.0 copy-done
  39.3 0.0 copy-done.2
  39.3 11.5 %tower.1 = (f32[2048,512]{1,0:T(8,128)}, f32[1,512]{1,0:T(1,128)}, f32[512,512]{1,0:T(8,128)}, f32[512,256]{1,0:T(8,128)}) custom-call(bf16[1024,512]{1,0:T(8,128)(2,1)S(1)} %get-tuple-element.11.hidden, bf16[2048,1024]{1,0:T(8,128)(2,1)} %get-tuple-element.12.turned, bf16[1024,1024]{1,0:T(8,128)(2,1)S(1)} %get-tuple-element.13.tallies, ...), custom_call_target="tpu_custom_call" | custom-call | flops 6442450944 | bytes 16777216 | tf_op jit(solution)/shard_map/tower/pallas_call | solution.py:465
Async XLA Ops:
  0.6 38.7 %copy-start.1 = (bf16[512,256]{1,0:T(8,128)(2,1)S(1)}, bf16[512,256]{1,0:T(8,128)(2,1)}, u32[]{:S(2)}) copy-start(bf16[512,256]{1,0:T(8,128)(2,1)} %w_out.1) | copy-start | bytes 786436
  0.6 38.7 %copy-start = (bf16[512,512]{1,0:T(8,128)(2,1)S(1)}, bf16[512,512]{1,0:T(8,128)(2,1)}, u32[]{:S(2)}) copy-start(bf16[512,512]{1,0:T(8,128)(2,1)} %w_in.1) | copy-start | bytes 1572868
  0.7 38.7 %copy-start.2 = (f32[512]{0:T(512)S(1)}, f32[512]{0:T(512)}, u32[]{:S(2)}) copy-start(f32[512]{0:T(512)} %param.11) | copy-start | bytes 6148

commit v5 on v4

--- a/solution.py
+++ b/solution.py
@@ -43,7 +43,10 @@
     return pl.ds(pl.multiple_of(start, size), size)
 
 
-STEPS = [(dx, dy) for dx in range(4) for dy in range(4) if dx or dy]
+STEPS = sorted(
+    ((dx, dy) for dx in range(4) for dy in range(4) if dx or dy),
+    key=lambda step: -min(step[0], 4 - step[0]) - min(step[1], 4 - step[1]),
+)
 
 
 def gather_kernel(

time: 50.9 us -> 49.7 us (0.976)
  Pallas kernels: 50.1 us -> 48.9 us
    pallas_call x1, Pallas kernels: 38.6 us -> 37.4 us  [gather_hidden(): pl.pallas_call(gather_kernel, name='gather_hidden', out_shape=(jax.ShapeD...]
where the time goes in v5:
time: 49.7 us; the launch traced here: 49.6 us
  Pallas kernels  48.9 us (98%)
  between operations  0.69 us (1%)
    pallas_call x1, Pallas kernels, gather_hidden(): pl.pallas_call(gather_kernel, name='gather_hidden', out_shape=(jax.ShapeD...  37.4 us
    pallas_call x1, Pallas kernels, tower(): pl.pallas_call(tower_kernel, name='tower', out_shape=(jax.ShapeDtypeStruc...  11.5 us

profile of v5, /device:TPU:1, one launch (start us, length us, event | category | flops | bytes accessed | tf_op | source)
XLA Modules:
  0.0 49.6 jit_solution(3739251391457887424)
XLA Ops:
  0.6 0.0 copy-start.1
  0.6 0.0 copy-start
  0.7 0.0 copy-start.2
  0.7 37.4 %gather_hidden.1 = (bf16[1024,512]{1,0:T(8,128)(2,1)S(1)}, bf16[2048,1024]{1,0:T(8,128)(2,1)}, bf16[1024,1024]{1,0:T(8,128)(2,1)S(1)}) custom-call(bf16[1024,2048]{1,0:T(8,128)(2,1)} %counts.1, s32[16,1024]{1,0:T(8,128)} %bitcast.4, s32[4,15]{1,0:T(4,128)} %neighbours.1, bf16[2048,512]{1,0:T(8,128)(2,1)} %weight.1), custom_call_target="tpu_custom_call" | custom-call | flops 2147483648 | bytes 16777216 | tf_op jit(solution)/shard_map/gather_hidden/pallas_call | solution.py:323
  38.1 0.0 copy-done.1
  38.1 0.0 copy-done
  38.1 0.0 copy-done.2
  38.1 11.5 %tower.1 = (f32[2048,512]{1,0:T(8,128)}, f32[1,512]{1,0:T(1,128)}, f32[512,512]{1,0:T(8,128)}, f32[512,256]{1,0:T(8,128)}) custom-call(bf16[1024,512]{1,0:T(8,128)(2,1)S(1)} %get-tuple-element.11.hidden, bf16[2048,1024]{1,0:T(8,128)(2,1)} %get-tuple-element.12.turned, bf16[1024,1024]{1,0:T(8,128)(2,1)S(1)} %get-tuple-element.13.tallies, ...), custom_call_target="tpu_custom_call" | custom-call | flops 6442450944 | bytes 16777216 | tf_op jit(solution)/shard_map/tower/pallas_call | solution.py:468
Async XLA Ops:
  0.6 37.5 %copy-start.1 = (bf16[512,256]{1,0:T(8,128)(2,1)S(1)}, bf16[512,256]{1,0:T(8,128)(2,1)}, u32[]{:S(2)}) copy-start(bf16[512,256]{1,0:T(8,128)(2,1)} %w_out.1) | copy-start | bytes 786436
  0.6 37.5 %copy-start = (bf16[512,512]{1,0:T(8,128)(2,1)S(1)}, bf16[512,512]{1,0:T(8,128)(2,1)}, u32[]{:S(2)}) copy-start(bf16[512,512]{1,0:T(8,128)(2,1)} %w_in.1) | copy-start | bytes 1572868
  0.7 37.5 %copy-start.2 = (f32[512]{0:T(512)S(1)}, f32[512]{0:T(512)}, u32[]{:S(2)}) copy-start(f32[512]{0:T(512)} %param.11) | copy-start | bytes 6148

commit v6 on v5

--- a/solution.py
+++ b/solution.py
@@ -69,7 +69,7 @@
     sibling = device(x, y, z, 1 - core)
     plane_to = [((x + dx) % 4, (y + dy) % 4) for dx, dy in STEPS]
     plane_device = [device(px, py, z, core) for px, py in plane_to]
-    column_device = [device(x, y, (z + step) % 8, core) for step in range(1, 8)]
+    column_device = [device(x, y, (z + step) % 8, core) for step in (4, 3, 5, 2, 6, 1, 7)]
 
     barrier = pltpu.get_barrier_semaphore()
     for other in [sibling] + plane_device + column_device:

time: 49.7 us -> 49.6 us (level)
  no operation moved by 1% of the time
where the time goes in v6:
time: 49.6 us
  Pallas kernels  48.9 us (99%)
  between operations  0.69 us (1%)
    pallas_call x1, Pallas kernels, gather_hidden(): pl.pallas_call(gather_kernel, name='gather_hidden', out_shape=(jax.ShapeD...  37.3 us
    pallas_call x1, Pallas kernels, tower(): pl.pallas_call(tower_kernel, name='tower', out_shape=(jax.ShapeDtypeStruc...  11.5 us

profile of v6, /device:TPU:1, one launch (start us, length us, event | category | flops | bytes accessed | tf_op | source)
XLA Modules:
  0.0 49.6 jit_solution(11922293716575687929)
XLA Ops:
  0.6 0.0 copy-start.1
  0.6 0.0 copy-start
  0.7 0.0 copy-start.2
  0.7 37.3 %gather_hidden.1 = (bf16[1024,512]{1,0:T(8,128)(2,1)S(1)}, bf16[2048,1024]{1,0:T(8,128)(2,1)}, bf16[1024,1024]{1,0:T(8,128)(2,1)S(1)}) custom-call(bf16[1024,2048]{1,0:T(8,128)(2,1)} %counts.1, s32[16,1024]{1,0:T(8,128)} %bitcast.4, s32[4,15]{1,0:T(4,128)} %neighbours.1, bf16[2048,512]{1,0:T(8,128)(2,1)} %weight.1), custom_call_target="tpu_custom_call" | custom-call | flops 2147483648 | bytes 16777216 | tf_op jit(solution)/shard_map/gather_hidden/pallas_call | solution.py:323
  38.0 0.0 copy-done.1
  38.0 0.0 copy-done
  38.0 0.0 copy-done.2
  38.0 11.5 %tower.1 = (f32[2048,512]{1,0:T(8,128)}, f32[1,512]{1,0:T(1,128)}, f32[512,512]{1,0:T(8,128)}, f32[512,256]{1,0:T(8,128)}) custom-call(bf16[1024,512]{1,0:T(8,128)(2,1)S(1)} %get-tuple-element.11.hidden, bf16[2048,1024]{1,0:T(8,128)(2,1)} %get-tuple-element.12.turned, bf16[1024,1024]{1,0:T(8,128)(2,1)S(1)} %get-tuple-element.13.tallies, ...), custom_call_target="tpu_custom_call" | custom-call | flops 6442450944 | bytes 16777216 | tf_op jit(solution)/shard_map/tower/pallas_call | solution.py:468
Async XLA Ops:
  0.6 37.4 %copy-start.1 = (bf16[512,256]{1,0:T(8,128)(2,1)S(1)}, bf16[512,256]{1,0:T(8,128)(2,1)}, u32[]{:S(2)}) copy-start(bf16[512,256]{1,0:T(8,128)(2,1)} %w_out.1) | copy-start | bytes 786436
  0.6 37.4 %copy-start = (bf16[512,512]{1,0:T(8,128)(2,1)S(1)}, bf16[512,512]{1,0:T(8,128)(2,1)}, u32[]{:S(2)}) copy-start(bf16[512,512]{1,0:T(8,128)(2,1)} %w_in.1) | copy-start | bytes 1572868
  0.7 37.4 %copy-start.2 = (f32[512]{0:T(512)S(1)}, f32[512]{0:T(512)}, u32[]{:S(2)}) copy-start(f32[512]{0:T(512)} %param.11) | copy-start | bytes 6148
